TPU v7x, 256 devices: a whole 4x4x8 slice. The times are simulated.
256 devices in a mesh: depth: 32 (over y, x, core), screen: 8 (over z).
Axes of the slice: x: 4, y: 4, z: 8, core: 2. Of those that a mesh axis runs over, the one named last changes fastest.
Arguments:
- density: bfloat16 [320, 768, 2048], P('depth', 'screen'), may hold values from 0.099609375 to 10
- material: int32 [256, 768, 2048], P('depth', 'screen'), may hold values from 0 to 15
- order: int32 [32], replicated, may hold values from 0 to 31, each once
- color_table: float32 [16, 3], replicated, may hold values from 0.3 to 3
- extinction: float32 [16], replicated, may hold values from 0.00390625 to 0.0390625
Outputs:
- image: float32 [4, 768, 2048], P(None, ('screen', 'depth'))
Inputs may be any that keep to these rules, and one draw needn't show every extreme that they name: order is a permutation: each brick has a distinct rank.
All inputs are finite; a program needn't handle non-finite values.
Results may differ from a plain program's by a relative error of at most 0.0003.
Values may be sent and summed in bfloat16 or wider, within the bound.
No kernel may reach another device: no remote copies, remote signals or barrier semaphores. Data moves between devices by JAX's collectives and lax.ppermute only.
A program may use at most 128 MiB of HBM per device.

v0:
```python
import jax
import jax.numpy as jnp
from jax import lax
from jax.sharding import PartitionSpec as P

light_x = 0.48
light_y = 0.6
light_z = 0.64


def with_halo(block, sides, width):
    for axis, dim in sides:
        count = lax.axis_size(axis)
        forward = [(i, i + 1) for i in range(count - 1)]
        backward = [(target, source) for source, target in forward]
        low = lax.ppermute(
            lax.slice_in_dim(block, block.shape[dim] - width, None, axis=dim), axis, forward
        )
        high = lax.ppermute(lax.slice_in_dim(block, 0, width, axis=dim), axis, backward)
        block = jnp.concatenate([low, block, high], axis=dim)
    return block


def lookup(kinds, table_column):
    picked = jnp.zeros(kinds.shape, jnp.float32)
    for entry in range(table_column.shape[0]):
        picked = jnp.where(kinds == entry, table_column[entry], picked)
    return picked


def body(density, material, order, color_table, extinction):
    with_rims = with_halo(density, (("screen", 1),), 1)
    float_full = with_rims.astype(jnp.float32)
    inner_rows = float_full[:, 1:-1]
    padded_x = jnp.pad(inner_rows, ((0, 0), (0, 0), (1, 1)))
    grad_z = 0.5 * (inner_rows[2:] - inner_rows[:-2])
    grad_y = 0.5 * (float_full[1:-1, 2:] - float_full[1:-1, :-2])
    grad_x = 0.5 * (padded_x[1:-1, :, 2:] - padded_x[1:-1, :, :-2])
    lit = light_x * grad_x + light_y * grad_y + light_z * grad_z
    shade = 0.55 + 0.45 * lit / jnp.sqrt(1.0 + grad_x * grad_x + grad_y * grad_y + grad_z * grad_z)
    rho = inner_rows[1:-1]
    extinct = lookup(material, extinction) * (rho / (1.0 + rho))
    ahead = jnp.cumsum(extinct, axis=0) - extinct
    weight = jnp.exp(-ahead) * (1.0 - jnp.exp(-extinct)) * shade
    red = jnp.sum(weight * lookup(material, color_table[:, 0]), axis=0)
    green = jnp.sum(weight * lookup(material, color_table[:, 1]), axis=0)
    blue = jnp.sum(weight * lookup(material, color_table[:, 2]), axis=0)
    optical = jnp.sum(extinct, axis=0)
    bricks = lax.axis_size("depth")
    rows = optical.shape[0]
    columns = optical.shape[1]
    strip_rows = rows // bricks
    before = (order[None, :] < order[:, None]).astype(jnp.float32)
    stacked = jnp.stack([red, green, blue, optical], axis=0).reshape(4, bricks, strip_rows, columns)
    strip_part = lax.all_to_all(stacked, "depth", split_axis=1, concat_axis=1, tiled=True)
    front_sum = jnp.einsum("kj,jrw->krw", before, strip_part[3], precision=lax.Precision.HIGHEST)
    attenuate = jnp.exp(-front_sum)
    colored = jnp.einsum(
        "ckrw,krw->crw", strip_part[:3], attenuate, precision=lax.Precision.HIGHEST
    )
    opacity_total = 1.0 - jnp.exp(-jnp.sum(strip_part[3], axis=0))
    return jnp.concatenate([colored, opacity_total[None]], axis=0)


def solution(mesh):
    placed = (P("depth", "screen", None), P("depth", "screen", None), P(), P(), P())
    return jax.shard_map(
        body,
        mesh=mesh,
        in_specs=placed,
        out_specs=P(None, ("screen", "depth"), None),
        check_vma=False,
    )
```

profile of v0, /device:TPU:97, one launch (start us, length us, event | category | flops | bytes accessed | tf_op | source)
XLA Modules:
  0.0 218.2 jit_solution(10330139608508704447)
XLA Ops:
  0.0 1.2 fusion.12
  1.2 4.8 %collective-permute-start = (bf16[10,1,2048]{2,1,0:T(2,128)(2,1)S(1)}, bf16[10,1,2048]{2,1,0:T(2,128)(2,1)S(1)}, u32[]{:S(2)}, u32[]{:S(2)}) collective-permute-start(bf16[10,1,2048]{2,1,0:T(2,128)(2,1)S(1)} %get-tuple-element.25), channel_id=1, source_target_pairs={{0,1},{1,2},{2,3},{3,4},{4,5},{5,6},{6,7},{8,9},{9,10},{10,11},{11... | collective-permute-start | bytes 122888 | tf_op jit(solution)/shard_map/ppermute | solution.py:16
  6.0 1.9 collective-permute-start.1
  7.9 2.1 fusion.15
  10.0 2.1 fusion.14
  12.1 2.0 fusion.17
  14.1 1.7 fusion.16
  15.8 0.0 collective-permute-done
  15.8 0.0 collective-permute-done.1
  15.8 3.1 %maximum_convert_fusion = f32[10,98,2048]{2,1,0:T(8,128)S(1)} fusion(bf16[10,1,2048]{2,1,0:T(2,128)(2,1)S(1)} %collective-permute-done.1, bf16[10,96,2048]{2,1,0:T(8,128)(2,1)} %param.5, bf16[10,1,2048]{2,1,0:T(2,128)(2,1)S(1)} %collective-permute-done), kind=kLoop, calls=%fused_computation.11 | loop fusion | flops 12042240 | bytes 12042240 | tf_op jit(solution)/shard_map/convert_element_type | solution.py:33
  18.9 0.0 copy-start
  18.9 4.7 %slice.408 = f32[10,96,2048]{2,1,0:T(8,128)} slice(f32[10,98,2048]{2,1,0:T(8,128)S(1)} %maximum_convert_fusion), slice={[0:10], [1:97], [0:2048]} | slice | bytes 15728640 | tf_op jit(solution)/shard_map/slice | solution.py:34
  23.6 0.9 copy-done
  24.5 35.2 %fusion.10 = (f32[96,2048]{1,0:T(8,128)}, f32[8,96,2048]{2,1,0:T(8,128)S(1)}, pred[8,96,2048]{2,1,0:T(8,128)(4,1)S(1)}, pred[8,96,2048]{2,1,0:T(8,128)(4,1)S(1)}...) fusion(f32[10,98,2048]{2,1,0:T(8,128)S(1)} %maximum_convert_fus, ...), kind=kLoop, calls=%fused_computation.43 | loop fusion | flops 56426496 | bytes 44826688 | tf_op jit(solution)/shard_map/reduce_sum | solution.py:48
  59.8 3.3 %fusion.18 = f32[8,96,2048]{2,1,0:T(8,128)} fusion(f32[8,96,2048]{2,1,0:T(8,128)S(1)} %get-tuple-element.8), kind=kOutput, calls=%fused_computation.50 | output fusion | flops 11010048 | bytes 12582912 | tf_op jit(solution)/shard_map/jit(cumsum)/reduce_window_sum | solution.py:43
  63.1 1.3 copy-done.1
  64.3 41.8 %multiply_reduce_fusion.2 = (f32[96,2048]{1,0:T(8,128)}, f32[8,96,2048]{2,1,0:T(8,128)}) fusion(pred[8,96,2048]{2,1,0:T(8,128)(4,1)} %get-tuple-element.24, pred[8,96,2048]{2,1,0:T(8,128)(4,1)} %get-tuple-element.23, pred[8,96,2048]{2,1,0:T(8,128)(4,1)} %get-tuple-element.22, pred[8,96,2048]{2,1,0:T(8,128)(4,1)} %get-tuple-element.21, ...), kind=kLoop, calls=%fused_computation.9 | loop fusion | flops 69009408 | bytes 77856832 | tf_op jit(solution)/shard_map/reduce_sum | solution.py:45
  106.1 23.9 %multiply_reduce_fusion.1 = f32[96,2048]{1,0:T(8,128)} fusion(f32[8,96,2048]{2,1,0:T(8,128)} %get-tuple-element.6, pred[8,96,2048]{2,1,0:T(8,128)(4,1)} %get-tuple-element.24, pred[8,96,2048]{2,1,0:T(8,128)(4,1)} %get-tuple-element.23, pred[8,96,2048]{2,1,0:T(8,128)(4,1)} %get-tuple-element.22, pred[8,96,2048]{2,1,0:T(8,128)(4,1)} %get-tuple-element.21, ...), kind=kLoop, calls=%fused_computation.8 | loop fusion | flops 28114944 | bytes 32243776 | tf_op jit(solution)/shard_map/reduce_sum | solution.py:46
  130.0 2.3 %stack.16 = f32[1,32,3,2048]{3,2,1,0:T(4,128)} reshape(f32[96,2048]{1,0:T(8,128)} %multiply_reduce_fusion.1) | data formatting | bytes 1572864 | tf_op jit(solution)/shard_map/stack | solution.py:54
  132.3 23.9 %multiply_reduce_fusion = f32[96,2048]{1,0:T(8,128)} fusion(f32[8,96,2048]{2,1,0:T(8,128)} %get-tuple-element.6, pred[8,96,2048]{2,1,0:T(8,128)(4,1)} %get-tuple-element.24, pred[8,96,2048]{2,1,0:T(8,128)(4,1)} %get-tuple-element.23, pred[8,96,2048]{2,1,0:T(8,128)(4,1)} %get-tuple-element.22, pred[8,96,2048]{2,1,0:T(8,128)(4,1)} %get-tuple-element.21, ...), kind=kLoop, calls=%fused_computation.7 | loop fusion | flops 28114944 | bytes 32243776 | tf_op jit(solution)/shard_map/reduce_sum | solution.py:47
  156.3 1.5 stack.17
  157.7 1.5 stack.15
  159.2 1.5 stack.18
  160.7 2.3 %pad_maximum_fusion = f32[4,32,3,2048]{3,2,1,0:T(4,128)S(1)} fusion(f32[1,32,3,2048]{3,2,1,0:T(4,128)S(1)} %stack.18, f32[1,32,3,2048]{3,2,1,0:T(4,128)S(1)} %stack.17, f32[1,32,3,2048]{3,2,1,0:T(4,128)} %stack.16, f32[1,32,3,2048]{3,2,1,0:T(4,128)S(1)} %stack.15), kind=kLoop, calls=%fused_computation.12 | loop fusion | flops 2359296 | bytes 6291456 | tf_op jit(solution)/shard_map/stack | solution.py:54
  163.0 0.0 copy-start.2
  163.1 3.3 %copy.7 = f32[4,32,3,2048]{3,0,2,1:T(4,128)S(1)} copy(f32[4,32,3,2048]{3,2,1,0:T(4,128)S(1)} %pad_maximum_fusion) | data formatting | bytes 6291456 | tf_op jit(solution)/shard_map/stack | solution.py:54
  166.3 47.4 %all_to_all.5 = f32[4,32,3,2048]{3,0,2,1:T(4,128)S(1)} all-to-all(f32[4,32,3,2048]{3,0,2,1:T(4,128)S(1)} %copy.7), channel_id=1, replica_groups=mesh['depth'=32,'screen'=8] {'depth'}, dimensions={1} | all-to-all | bytes 6291456 | tf_op jit(solution)/shard_map/all_to_all | solution.py:55
  213.7 1.0 fusion.13
  214.7 0.8 fusion.5
  215.5 0.5 copy.18
  216.1 1.4 fusion.3
  217.5 0.7 pad_maximum_fusion.1
  (4 shorter events, 0.0 us)
Async XLA Ops:
  1.2 14.6 %collective-permute-start = (bf16[10,1,2048]{2,1,0:T(2,128)(2,1)S(1)}, bf16[10,1,2048]{2,1,0:T(2,128)(2,1)S(1)}, u32[]{:S(2)}, u32[]{:S(2)}) collective-permute-start(bf16[10,1,2048]{2,1,0:T(2,128)(2,1)S(1)} %get-tuple-element.25), channel_id=1, source_target_pairs={{0,1},{1,2},{2,3},{3,4},{4,5},{5,6},{6,7},{8,9},{9,10},{10,11},{11... | collective-permute-start | bytes 122888 | tf_op jit(solution)/shard_map/ppermute | solution.py:16
  6.0 9.8 %collective-permute-start.1 = (bf16[10,1,2048]{2,1,0:T(2,128)(2,1)S(1)}, bf16[10,1,2048]{2,1,0:T(2,128)(2,1)S(1)}, u32[]{:S(2)}, u32[]{:S(2)}) collective-permute-start(bf16[10,1,2048]{2,1,0:T(2,128)(2,1)S(1)} %get-tuple-element.26), channel_id=1, source_target_pairs={{1,0},{2,1},{3,2},{4,3},{5,4},{6,5},{7,6},{9,8},{10,9},{11,10},{12... | collective-permute-start | bytes 122888 | tf_op jit(solution)/shard_map/ppermute | solution.py:19
  18.9 5.6 %copy-start = (f32[10,98,2048]{2,1,0:T(8,128)}, f32[10,98,2048]{2,1,0:T(8,128)S(1)}, u32[]{:S(2)}) copy-start(f32[10,98,2048]{2,1,0:T(8,128)S(1)} %maximum_convert_fusion) | copy-start | bytes 24084484
  59.8 4.6 %copy-start.1 = (f32[8,96,2048]{2,1,0:T(8,128)}, f32[8,96,2048]{2,1,0:T(8,128)S(1)}, u32[]{:S(2)}) copy-start(f32[8,96,2048]{2,1,0:T(8,128)S(1)} %get-tuple-element.8) | copy-start | bytes 18874372
  163.0 51.7 %copy-start.2 = (s32[32]{0:T(128)S(1)}, s32[32]{0:T(128)}, u32[]{:S(2)}) copy-start(s32[32]{0:T(128)} %param.7) | copy-start | bytes 388
where the time goes:
time: 219 us; the launch traced here: 218 us
  other arithmetic  137 us (63%)
  blocking collectives  47.4 us (22%)
  local copies, waits for them, and re-layouts  26.6 us (12%)
  starting transfers between devices  6.68 us (3%)
    all_to_all x1, blocking collectives, body(): lax.all_to_all(stacked, 'depth', split_axis=1, concat_axis=1, tiled=True)  47.4 us
    reduce_sum x1, other arithmetic, body(): red = jnp.sum(weight * lookup(material, color_table[:, 0]), axis=0)  41.8 us
    reduce_sum x1, other arithmetic, body(): optical = jnp.sum(extinct, axis=0)  35.2 us
    reduce_sum x1, other arithmetic, body(): blue = jnp.sum(weight * lookup(material, color_table[:, 2]), axis=0)  23.9 us
    reduce_sum x1, other arithmetic, body(): green = jnp.sum(weight * lookup(material, color_table[:, 1]), axis=0)  23.9 us
    another operation x5, local copies, waits for them, and re-layouts, body(): jnp.stack([red, green, blue, optical], axis=0)  9.99 us
    slice x4, local copies, waits for them, and re-layouts, lookup(): picked = jnp.where(kinds == entry, table_column[entry], picked)  7.89 us
    ppermute x1, starting transfers between devices, with_halo(): lax.ppermute(lax.slice_in_dim(block, block.shape[dim] - width, None, axis...  4.76 us
  transfers between devices with their start and end apart: 2, of which 0 were waited for; matrix products, arithmetic and copies ran while one was open for 4% of the time, Pallas kernels for 0%

commit v1 on v0

v1 whole, which is shorter than its diff:
```python
import functools
import math

import jax
import jax.numpy as jnp
from jax import lax
from jax.experimental import pallas as pl
from jax.experimental.pallas import tpu as pltpu
from jax.sharding import PartitionSpec as P

light_x = 0.48
light_y = 0.6
light_z = 0.64
ambient = 0.55
diffuse = 0.45

LANES = 128
SUB = 8
CB = 256
PER = CB // LANES
LOG2E = math.log2(math.e)

SLICES = 8
TAU_TOP = SLICES * 0.0390625 * (10.0 / 11.0) * LOG2E * 1.001
LOG_TOP = 0.0
LOG_LOW = -14.0
LEVELS = 65535.0
TAU_STEP = TAU_TOP / LEVELS
LOG_STEP = (LOG_TOP - LOG_LOW) / LEVELS


def quantize(value, low, step):
    level = (value - low) * (1.0 / step) + 0.5
    return jnp.clip(level, 0.0, LEVELS).astype(jnp.int32)


def pick(low_table, high_table, index, upper):
    low = jnp.take_along_axis(low_table, index, axis=0)
    high = jnp.take_along_axis(high_table, index, axis=0)
    return jnp.where(upper, high, low)


def shade_kernel(blocks, left_ref, mid_ref, right_ref, low_ref, high_ref, mat_ref, tab_ref, band_ref, out_ref, full, diff):
    step = pl.program_id(0)
    ghost, rows = mid_ref.shape[0], mid_ref.shape[1]
    slices = ghost - 2
    for z in range(ghost):
        for c in range(PER):
            cols = pl.ds(c * LANES, LANES)
            full[z, c, SUB : SUB + rows, :] = mid_ref[z, :, cols].astype(jnp.float32)
            full[z, c, SUB - 1 : SUB, :] = low_ref[z, :, cols].astype(jnp.float32)
            full[z, c, SUB + rows : SUB + rows + 1, :] = high_ref[z, :, cols].astype(jnp.float32)
    window = jnp.concatenate([left_ref[1:-1], mid_ref[1:-1], right_ref[1:-1]], axis=-1)
    diff[...] = jnp.dot(
        window.reshape(slices * rows, CB + 2 * LANES), band_ref[0], preferred_element_type=jnp.float32
    ).reshape(slices, rows, CB)
    tables = [tab_ref[i] for i in range(8)]
    stride = 2 * blocks

    def row_block(r, carry):
        base = pl.multiple_of(r * SUB, SUB)
        for c in range(PER):
            cols = pl.ds(c * LANES, LANES)
            through = jnp.ones((SUB, LANES), jnp.float32)
            depth = jnp.zeros((SUB, LANES), jnp.float32)
            sums = [jnp.zeros((SUB, LANES), jnp.float32) for _ in range(3)]
            for z in range(slices):
                rho = full[z + 1, c, pl.ds(base + SUB, SUB), :]
                dz = full[z + 2, c, pl.ds(base + SUB, SUB), :] - full[z, c, pl.ds(base + SUB, SUB), :]
                dy = full[z + 1, c, pl.ds(base + SUB + 1, SUB), :] - full[z + 1, c, pl.ds(base + SUB - 1, SUB), :]
                dx = diff[z, pl.ds(base, SUB), cols]
                lit = (diffuse * light_x) * dx + (diffuse * light_y) * dy + (diffuse * light_z) * dz
                shade = ambient + lit * lax.rsqrt(4.0 + dx * dx + dy * dy + dz * dz)
                kind = mat_ref[z, pl.ds(base, SUB), cols]
                upper = kind >= SUB
                index = kind & (SUB - 1)
                depth = depth + pick(tables[0], tables[1], index, upper) * (rho / (1.0 + rho))
                after = jnp.exp2(-depth)
                weight = (through - after) * shade
                through = after
                for channel in range(3):
                    sums[channel] = sums[channel] + weight * pick(
                        tables[2 + 2 * channel], tables[3 + 2 * channel], index, upper
                    )
            red, green, blue = (quantize(jnp.log2(value), LOG_LOW, LOG_STEP) for value in sums)
            deep = quantize(depth, 0.0, TAU_STEP)
            spot = base * stride + step * PER + c
            out_ref[pl.ds(spot, SUB, stride=stride), :] = (red << 16) | green
            out_ref[pl.ds(spot + blocks, SUB, stride=stride), :] = (blue << 16) | deep
        return carry

    lax.fori_loop(0, rows // SUB, row_block, 0)


def shade_bricks(density, low, high, material, tables, band):
    ghost, rows, columns = density.shape
    slices = material.shape[0]
    steps = columns // CB
    blocks = columns // LANES
    return pl.pallas_call(
        functools.partial(shade_kernel, blocks),
        grid=(steps,),
        in_specs=[
            pl.BlockSpec((ghost, rows, LANES), lambda i: (0, 0, jnp.maximum(PER * i - 1, 0))),
            pl.BlockSpec((ghost, rows, CB), lambda i: (0, 0, i)),
            pl.BlockSpec((ghost, rows, LANES), lambda i: (0, 0, jnp.minimum(PER * i + PER, blocks - 1))),
            pl.BlockSpec((ghost, 1, CB), lambda i: (0, 0, i)),
            pl.BlockSpec((ghost, 1, CB), lambda i: (0, 0, i)),
            pl.BlockSpec((slices, rows, CB), lambda i: (0, 0, i)),
            pl.BlockSpec((8, SUB, LANES), lambda i: (0, 0, 0)),
            pl.BlockSpec(
                (1, CB + 2 * LANES, CB),
                lambda i: (jnp.where(i == 0, 0, jnp.where(i == steps - 1, 2, 1)), 0, 0),
            ),
        ],
        out_specs=pl.BlockSpec((rows * 2 * blocks, LANES), lambda i: (0, 0)),
        out_shape=jax.ShapeDtypeStruct((rows * 2 * blocks, LANES), jnp.int32),
        scratch_shapes=[
            pltpu.VMEM((ghost, PER, rows + 2 * SUB, LANES), jnp.float32),
            pltpu.VMEM((slices, rows, CB), jnp.float32),
        ],
        compiler_params=pltpu.CompilerParams(vmem_limit_bytes=56 << 20),
    )(density, density, density, low, high, material, tables, band)


def blend_kernel(order_ref, part_ref, out_ref, place, image):
    bricks, rows, pairs, blocks, lanes = part_ref.shape
    for brick in range(bricks):
        place[order_ref[brick]] = brick
    for row in range(rows):
        for group in range(blocks // SUB):
            spots = pl.ds(group * SUB, SUB)

            def walk(rank, carry, row=row, spots=spots):
                front, red, green, blue = carry
                brick = place[rank]
                first = part_ref[brick, row, 0, spots, :]
                second = part_ref[brick, row, 1, spots, :]

                def seen(code):
                    return jnp.exp2(code.astype(jnp.float32) * LOG_STEP + (LOG_LOW - front))

                red = red + seen(lax.shift_right_logical(first, 16))
                green = green + seen(first & 0xFFFF)
                blue = blue + seen(lax.shift_right_logical(second, 16))
                front = front + (second & 0xFFFF).astype(jnp.float32) * TAU_STEP
                return front, red, green, blue

            zero = jnp.zeros((SUB, lanes), jnp.float32)
            front, red, green, blue = lax.fori_loop(0, bricks, walk, (zero,) * 4, unroll=4)
            for channel, value in enumerate((red, green, blue, 1.0 - jnp.exp2(-front))):
                image[pl.ds((row * 4 + channel) * blocks + group * SUB, SUB), :] = value
        for block in range(blocks):
            out_ref[row, :, pl.ds(block * lanes, lanes)] = image[pl.ds(row * 4 * blocks + block, 4, stride=blocks), :]


def blend(order, part):
    bricks, rows, pairs, blocks, lanes = part.shape
    return pl.pallas_call(
        blend_kernel,
        in_specs=[pl.BlockSpec(memory_space=pltpu.SMEM), pl.BlockSpec(memory_space=pltpu.VMEM)],
        out_specs=pl.BlockSpec(memory_space=pltpu.VMEM),
        out_shape=jax.ShapeDtypeStruct((rows, 4, blocks * lanes), jnp.float32),
        scratch_shapes=[pltpu.SMEM((bricks,), jnp.int32), pltpu.VMEM((rows * 4 * blocks, lanes), jnp.float32)],
    )(order, part)


def band_matrices():
    source = jnp.arange(CB + 2 * LANES)[:, None] - LANES
    target = jnp.arange(CB)[None, :]
    inner = (source == target + 1).astype(jnp.float32) - (source == target - 1).astype(jnp.float32)
    first = jnp.where(source < 0, 0.0, inner)
    last = jnp.where(source >= CB, 0.0, inner)
    return jnp.stack([first, inner, last]).astype(jnp.bfloat16)


def body(density, material, order, color_table, extinction):
    count = lax.axis_size("screen")
    rows, columns = density.shape[1], density.shape[2]
    bricks = lax.axis_size("depth")
    forward = [(i, i + 1) for i in range(count - 1)]
    backward = [(target, source) for source, target in forward]
    low = lax.ppermute(density[:, rows - 1 :], "screen", forward)
    high = lax.ppermute(density[:, :1], "screen", backward)
    entries = jnp.concatenate([(LOG2E * extinction)[None], color_table.T], axis=0)
    tables = jnp.broadcast_to(entries.reshape(8, SUB, 1), (8, SUB, LANES))
    coded = shade_bricks(density, low, high, material, tables, band_matrices())
    blocks = columns // LANES
    strip = rows // bricks
    parts = coded.reshape(bricks, strip * 2 * blocks, LANES)
    parts = lax.all_to_all(parts, "depth", split_axis=0, concat_axis=0, tiled=True)
    image = blend(order, parts.reshape(bricks, strip, 2, blocks, LANES))
    return image.transpose(1, 0, 2)


def solution(mesh):
    placed = (P("depth", "screen", None), P("depth", "screen", None), P(), P(), P())
    return jax.shard_map(
        body,
        mesh=mesh,
        in_specs=placed,
        out_specs=P(None, ("screen", "depth"), None),
        check_vma=False,
    )
```

time: 219 us -> 66.1 us (0.30)
  other arithmetic: 137 us -> 2.61 us
  local copies, waits for them, and re-layouts: 26.6 us -> 1.97 us
  Pallas kernels: 0 us -> 23.6 us
  blocking collectives: 47.4 us -> 30.9 us
    reduce_sum x4 -> x0, other arithmetic: 125 us -> none  [the longest x1 41.8 us: body(): red = jnp.sum(weight * lookup(material, color_table[:, 0]), axis=0)]
    pallas_call x0 -> x2, Pallas kernels: none -> 23.6 us  [the longest x1 20.3 us: shade_bricks(): pl.pallas_call(functools.partial(shade_kernel, blocks), grid=(steps,), in...]
    all_to_all x1, blocking collectives: 47.4 us -> 30.9 us  [body(): lax.all_to_all(parts, 'depth', split_axis=0, concat_axis=0, tiled=True)]
    slice x6 -> x1, local copies, waits for them, and re-layouts: 13.8 us -> 1.2 us  [body(): high = lax.ppermute(density[:, :1], 'screen', backward)]
    another operation x5 -> x0, local copies, waits for them, and re-layouts: 9.99 us -> none  [body(): jnp.stack([red, green, blue, optical], axis=0)]
    another operation x2, other arithmetic: 5.65 us -> 1.24 us  [the longest x1 0.97 us: band_matrices(): return jnp.stack([first, inner, last]).astype(jnp.bfloat16)]
    convert_element_type x1 -> x0, other arithmetic: 3.06 us -> none  [body(): float_full = with_rims.astype(jnp.float32)]
    unnamed x7 -> x4, local copies, waits for them, and re-layouts: 2.77 us -> 0.01 us
where the time goes in v1:
time: 66.1 us; the launch traced here: 65.8 us
  blocking collectives  30.9 us (47%)
  Pallas kernels  23.6 us (36%)
  starting transfers between devices  6.68 us (10%)
  other arithmetic  2.61 us (4%)
  local copies, waits for them, and re-layouts  1.97 us (3%)
    all_to_all x1, blocking collectives, body(): lax.all_to_all(parts, 'depth', split_axis=0, concat_axis=0, tiled=True)  30.9 us
    pallas_call x1, Pallas kernels, shade_bricks(): pl.pallas_call(functools.partial(shade_kernel, blocks), grid=(steps,), in...  20.3 us
    ppermute x1, starting transfers between devices, body(): low = lax.ppermute(density[:, rows - 1:], 'screen', forward)  4.76 us
    pallas_call x1, Pallas kernels, blend(): pl.pallas_call(blend_kernel, in_specs=[pl.BlockSpec(memory_space=pltpu.SM...  3.33 us
    ppermute x1, starting transfers between devices, body(): high = lax.ppermute(density[:, :1], 'screen', backward)  1.92 us
  transfers between devices with their start and end apart: 2, of which 0 were waited for; matrix products, arithmetic and copies ran while one was open for 4% of the time, Pallas kernels for 0%

profile of v1, /device:TPU:97, one launch (start us, length us, event | category | flops | bytes accessed | tf_op | source)
XLA Modules:
  0.0 65.8 jit_solution(14619118507055870338)
XLA Ops:
  0.0 1.2 %fusion.3 = (bf16[10,1,2048]{2,1,0:T(2,128)(2,1)S(1)}, bf16[10,1,2048]{2,1,0:T(2,128)(2,1)S(1)}) fusion(bf16[10,96,2048]{2,1,0:T(8,128)(2,1)} %right_ref.1), kind=kLoop, calls=%fused_computation.12 | loop fusion | bytes 163840 | tf_op jit(solution)/shard_map/slice | solution.py:184
  1.2 1.9 %collective-permute-start.1 = (bf16[10,1,2048]{2,1,0:T(2,128)(2,1)S(1)}, bf16[10,1,2048]{2,1,0:T(2,128)(2,1)S(1)}, u32[]{:S(2)}, u32[]{:S(2)}) collective-permute-start(bf16[10,1,2048]{2,1,0:T(2,128)(2,1)S(1)} %get-tuple-element.5), channel_id=1, source_target_pairs={{1,0},{2,1},{3,2},{4,3},{5,4},{6,5},{7,6},{9,8},{10,9},{11,10},{12... | collective-permute-start | bytes 122888 | tf_op jit(solution)/shard_map/ppermute | solution.py:184
  3.1 4.8 %collective-permute-start = (bf16[10,1,2048]{2,1,0:T(2,128)(2,1)S(1)}, bf16[10,1,2048]{2,1,0:T(2,128)(2,1)S(1)}, u32[]{:S(2)}, u32[]{:S(2)}) collective-permute-start(bf16[10,1,2048]{2,1,0:T(2,128)(2,1)S(1)} %get-tuple-element.6), channel_id=1, source_target_pairs={{0,1},{1,2},{2,3},{3,4},{4,5},{5,6},{6,7},{8,9},{9,10},{10,11},{11... | collective-permute-start | bytes 122888 | tf_op jit(solution)/shard_map/ppermute | solution.py:183
  7.9 0.7 %multiply_bitcast_fusion = f32[1,16]{1,0:T(1,128)S(1)} fusion(f32[16]{0:T(128)} %param.9), kind=kLoop, calls=%fused_computation.11 | loop fusion | flops 16 | bytes 128 | tf_op jit(solution)/shard_map/broadcast_in_dim | solution.py:185
  8.6 0.3 select_convert_fusion.1
  8.9 1.0 %pad_maximum_fusion.band_ref = bf16[3,512,256]{2,1,0:T(8,128)(2,1)} fusion(bf16[1,512,256]{2,1,0:T(8,128)(2,1)S(1)} %get-tuple-element.9, bf16[1,512,256]{2,1,0:T(8,128)(2,1)S(1)} %get-tuple-element.8, bf16[1,512,256]{2,1,0:T(8,128)(2,1)S(1)} %get-tuple-element.7), kind=kLoop, calls=%fused_computation | loop fusion | flops 786432 | bytes 1572864 | tf_op jit(solution)/shard_map/stack | solution.py:174
  9.8 0.7 %pad_maximum_fusion.1 = f32[4,16]{1,0:T(4,128)S(1)} fusion(f32[3,16]{1,0:T(4,128)} %bitcast.8, f32[1,16]{1,0:T(1,128)S(1)} %multiply_bitcast_fusion), kind=kLoop, calls=%fused_computation.5 | loop fusion | flops 64 | bytes 512 | tf_op jit(solution)/shard_map/concatenate | solution.py:185
  10.5 0.1 broadcast_in_dim.31
  10.6 0.0 collective-permute-done.1.high_ref
  10.6 0.0 copy-start
  10.6 0.0 collective-permute-done.low_ref
  10.6 0.0 copy-start.1
  10.6 0.7 %broadcast_in_dim.32.tab_ref = f32[8,8,128]{2,1,0:T(8,128)} broadcast(f32[8,8]{1,0:T(8,128)S(1)} %broadcast_in_dim.31), dimensions={0,1} | broadcast | bytes 33024 | tf_op jit(solution)/shard_map/broadcast_in_dim | solution.py:186
  11.3 0.0 copy-done
  11.3 0.0 copy-done.1
  11.3 20.3 %shard_map.55 = s32[3072,128]{1,0:T(8,128)} custom-call(bf16[10,96,2048]{2,1,0:T(8,128)(2,1)} %right_ref.1, bf16[10,96,2048]{2,1,0:T(8,128)(2,1)} %right_ref.1, bf16[10,96,2048]{2,1,0:T(8,128)(2,1)} %right_ref.1, bf16[10,1,2048]{2,1,0:T(2,128)(2,1)} %copy-done.1, bf16[10,1,2048]{2,1,0:T(2,128)(2,1)} %copy-done, s32[8,96,2048]{2,1,0:T(8,128)} %mat_ref.1, ...), custom_call_target="tpu_custom_call" | custom-call | tf_op jit(solution)/shard_map/pallas_call | solution.py:100
  31.6 30.9 %all_to_all.5 = s32[32,96,128]{2,1,0:T(8,128)} all-to-all(s32[32,96,128]{2,1,0:T(8,128)} %bitcast.6), channel_id=1, replica_groups=mesh['depth'=32,'screen'=8] {'depth'}, dimensions={0} | all-to-all | bytes 3145728 | tf_op jit(solution)/shard_map/all_to_all | solution.py:191
  62.5 3.3 %shard_map.56 = f32[3,4,2048]{2,1,0:T(4,128)} custom-call(s32[32]{0:T(128)} %order_ref.1, s32[32,3,2,16,128]{4,3,2,1,0:T(8,128)} %bitcast.7), custom_call_target="tpu_custom_call" | custom-call | tf_op jit(solution)/shard_map/pallas_call | solution.py:159
  (3 shorter events, 0.0 us)
Async XLA Ops:
  1.2 9.4 %collective-permute-start.1 = (bf16[10,1,2048]{2,1,0:T(2,128)(2,1)S(1)}, bf16[10,1,2048]{2,1,0:T(2,128)(2,1)S(1)}, u32[]{:S(2)}, u32[]{:S(2)}) collective-permute-start(bf16[10,1,2048]{2,1,0:T(2,128)(2,1)S(1)} %get-tuple-element.5), channel_id=1, source_target_pairs={{1,0},{2,1},{3,2},{4,3},{5,4},{6,5},{7,6},{9,8},{10,9},{11,10},{12... | collective-permute-start | bytes 122888 | tf_op jit(solution)/shard_map/ppermute | solution.py:184
  3.1 7.5 %collective-permute-start = (bf16[10,1,2048]{2,1,0:T(2,128)(2,1)S(1)}, bf16[10,1,2048]{2,1,0:T(2,128)(2,1)S(1)}, u32[]{:S(2)}, u32[]{:S(2)}) collective-permute-start(bf16[10,1,2048]{2,1,0:T(2,128)(2,1)S(1)} %get-tuple-element.6), channel_id=1, source_target_pairs={{0,1},{1,2},{2,3},{3,4},{4,5},{5,6},{6,7},{8,9},{9,10},{10,11},{11... | collective-permute-start | bytes 122888 | tf_op jit(solution)/shard_map/ppermute | solution.py:183
  10.6 0.7 %copy-start = (bf16[10,1,2048]{2,1,0:T(2,128)(2,1)}, bf16[10,1,2048]{2,1,0:T(2,128)(2,1)S(1)}, u32[]{:S(2)}) copy-start(bf16[10,1,2048]{2,1,0:T(2,128)(2,1)S(1)} %collective-permute-done.1.high_ref) | copy-start | bytes 122884
  10.6 0.7 %copy-start.1 = (bf16[10,1,2048]{2,1,0:T(2,128)(2,1)}, bf16[10,1,2048]{2,1,0:T(2,128)(2,1)S(1)}, u32[]{:S(2)}) copy-start(bf16[10,1,2048]{2,1,0:T(2,128)(2,1)S(1)} %collective-permute-done.low_ref) | copy-start | bytes 122884

commit v2 on v1

v2 whole, which is shorter than its diff:
```python
import functools
import math

import jax
import jax.numpy as jnp
from jax import lax
from jax.experimental import pallas as pl
from jax.experimental.pallas import tpu as pltpu
from jax.sharding import PartitionSpec as P

light_x = 0.48
light_y = 0.6
light_z = 0.64
ambient = 0.55
diffuse = 0.45

LANES = 128
SUB = 8
CB = 256
PER = CB // LANES
CHUNK = 32
LANE_TABLES = 1
LOG2E = math.log2(math.e)

SLICES = 8
TAU_TOP = SLICES * 0.0390625 * (10.0 / 11.0) * LOG2E * 1.001
LOG_TOP = 0.0
LOG_LOW = -14.0
LEVELS = 65535.0
TAU_STEP = TAU_TOP / LEVELS
LOG_STEP = (LOG_TOP - LOG_LOW) / LEVELS


def quantize(value, low, step):
    return (value * (1.0 / step) + (0.5 - low / step)).astype(jnp.int32)


def entries_at(table, index):
    numbers = lax.GatherDimensionNumbers(
        offset_dims=(),
        collapsed_slice_dims=(0,),
        start_index_map=(0,),
        operand_batching_dims=(1,),
        start_indices_batching_dims=(1,),
    )
    return lax.gather(
        table, index[..., None], numbers, (1, 1), mode=lax.GatherScatterMode.PROMISE_IN_BOUNDS
    )


def lane_entries(table, index):
    numbers = lax.GatherDimensionNumbers(
        offset_dims=(),
        collapsed_slice_dims=(1,),
        start_index_map=(1,),
        operand_batching_dims=(0,),
        start_indices_batching_dims=(0,),
    )
    return lax.gather(
        table, index[..., None], numbers, (1, 1), mode=lax.GatherScatterMode.PROMISE_IN_BOUNDS
    )


def pick(low_table, high_table, index, upper):
    return jnp.where(upper, entries_at(high_table, index), entries_at(low_table, index))


def shade_kernel(den_hbm, low_ref, high_ref, mat_hbm, color_hbm, ext_hbm, out_ref, den, mat, full, diff, table, band, color_ref, ext_ref, den_sem, mat_sem, table_sem):
    ghost, rows, columns = den.shape
    slices = ghost - 2
    steps = columns // CB
    blocks = columns // LANES
    stride = 2 * blocks

    def den_copy(j):
        cols = pl.ds(pl.multiple_of(j * CB, CB), CB)
        return pltpu.make_async_copy(den_hbm.at[:, :, cols], den.at[:, :, cols], den_sem.at[j])

    def mat_copy(j):
        cols = pl.ds(pl.multiple_of(j * CB, CB), CB)
        return pltpu.make_async_copy(mat_hbm.at[:, :, cols], mat.at[:, :, cols], mat_sem.at[j])

    color_copy = pltpu.make_async_copy(color_hbm, color_ref, table_sem.at[0])
    ext_copy = pltpu.make_async_copy(ext_hbm, ext_ref, table_sem.at[1])
    color_copy.start()
    ext_copy.start()
    den_copy(0).start()
    den_copy(1).start()
    for j in range(steps):
        mat_copy(j).start()
        if j + 2 < steps:
            den_copy(j + 2).start()

    source = lax.broadcasted_iota(jnp.int32, (2 * SUB, LANES), 0)
    target = lax.broadcasted_iota(jnp.int32, (2 * SUB, LANES), 1)
    for top in range(0, CB + 2 * LANES, 2 * SUB):
        for side in range(0, CB, LANES):
            shift = (source + (top - LANES)) - (target + side)
            tile = (shift == 1).astype(jnp.float32) - (shift == -1).astype(jnp.float32)
            band[top : top + 2 * SUB, side : side + LANES] = tile.astype(jnp.bfloat16)
    color_copy.wait()
    ext_copy.wait()
    lane = lax.broadcasted_iota(jnp.int32, (SUB, LANES), 1)
    for channel in range(LANE_TABLES):
        spread = jnp.zeros((SUB, LANES), jnp.float32)
        for entry in range(2 * SUB):
            spread = jnp.where(lane == entry, (diffuse * light_x) * color_ref[channel, entry], spread)
        table[2 + 2 * channel] = spread
    for entry in range(SUB):
        for half in range(2):
            spot = entry + half * SUB
            table[half, entry : entry + 1, :] = jnp.full((1, LANES), -LOG2E * ext_ref[spot], jnp.float32)
            for channel in range(LANE_TABLES, 3):
                scale = (diffuse * light_x) * color_ref[channel, spot]
                table[2 + 2 * channel + half, entry : entry + 1, :] = jnp.full((1, LANES), scale, jnp.float32)
    tables = [table[i] for i in range(8)]

    def shade_columns(j, carry):
        @pl.when(j + 1 < steps)
        def _():
            den_copy(j + 1).wait()

        mat_copy(j).wait()
        start = pl.multiple_of(j * CB, CB)
        left = pl.multiple_of(jnp.maximum(start - LANES, 0), LANES)
        right = pl.multiple_of(jnp.minimum(start + CB, columns - LANES), LANES)
        inside_left = jnp.where(j == 0, 0.0, 1.0).astype(jnp.bfloat16)
        inside_right = jnp.where(j == steps - 1, 0.0, 1.0).astype(jnp.bfloat16)

        def fill(r):
            for z in range(ghost):
                for c in range(PER):
                    cols = pl.ds(start + c * LANES, LANES)
                    if r == 0:
                        full[z, c, SUB - 1 : SUB, :] = low_ref[z, :, cols].astype(jnp.float32)
                    full[z, c, pl.ds(SUB + r * CHUNK, CHUNK), :] = den[z, pl.ds(r * CHUNK, CHUNK), cols].astype(jnp.float32)
                    if r == rows // CHUNK - 1:
                        full[z, c, SUB + rows : SUB + rows + 1, :] = high_ref[z, :, cols].astype(jnp.float32)

        def across(r):
            spots = pl.ds(r * CHUNK, CHUNK)
            window = jnp.concatenate(
                [
                    den[1:-1, spots, pl.ds(left, LANES)] * inside_left,
                    den[1:-1, spots, pl.ds(start, CB)],
                    den[1:-1, spots, pl.ds(right, LANES)] * inside_right,
                ],
                axis=-1,
            )
            diff[:, spots, :] = jnp.dot(
                window.reshape(slices * CHUNK, CB + 2 * LANES), band[...], preferred_element_type=jnp.float32
            ).reshape(slices, CHUNK, CB)

        def shade_tile(base, c):
            spots = pl.ds(base, SUB)
            through = jnp.ones((SUB, LANES), jnp.float32)
            depth = jnp.zeros((SUB, LANES), jnp.float32)
            sums = [jnp.zeros((SUB, LANES), jnp.float32) for _ in range(3)]
            for z in range(slices):
                rho = full[z + 1, c, pl.ds(base + SUB, SUB), :]
                dz = full[z + 2, c, pl.ds(base + SUB, SUB), :] - full[z, c, pl.ds(base + SUB, SUB), :]
                dy = full[z + 1, c, pl.ds(base + SUB + 1, SUB), :] - full[z + 1, c, pl.ds(base + SUB - 1, SUB), :]
                dx = diff[z, spots, pl.ds(c * LANES, LANES)]
                lit = dx + (light_y / light_x) * dy + (light_z / light_x) * dz
                bend = lax.rsqrt(4.0 + dx * dx + dy * dy + dz * dz)
                shade = ambient / (diffuse * light_x) + lit * bend
                kind = mat[z, spots, pl.ds(start + c * LANES, LANES)]
                upper = kind >= SUB
                index = kind & (SUB - 1)
                depth = depth + pick(tables[0], tables[1], index, upper) * (rho * (1.0 / (1.0 + rho)))
                after = jnp.exp2(depth)
                weight = (through - after) * shade
                through = after
                for channel in range(3):
                    if channel < LANE_TABLES:
                        color = lane_entries(tables[2 + 2 * channel], kind)
                    else:
                        color = pick(tables[2 + 2 * channel], tables[3 + 2 * channel], index, upper)
                    sums[channel] = sums[channel] + weight * color
            red, green, blue = (quantize(jnp.log2(value), LOG_LOW, LOG_STEP) for value in sums)
            deep = quantize(depth, 0.0, -TAU_STEP)
            spot = base * stride + j * PER + c
            out_ref[pl.ds(spot, SUB, stride=stride), :] = (red << 16) | green
            out_ref[pl.ds(spot + blocks, SUB, stride=stride), :] = (blue << 16) | deep

        chunks = rows // CHUNK
        fill(0)
        across(0)
        for r in range(chunks):
            if r + 1 < chunks:
                fill(r + 1)
                across(r + 1)
            for base in range(r * CHUNK, (r + 1) * CHUNK, SUB):
                for c in range(PER):
                    shade_tile(base, c)
        return carry

    den_copy(0).wait()
    lax.fori_loop(0, steps, shade_columns, 0)


def shade_bricks(density, low, high, material, color_table, extinction):
    ghost, rows, columns = density.shape
    slices = material.shape[0]
    steps = columns // CB
    blocks = columns // LANES
    return pl.pallas_call(
        shade_kernel,
        in_specs=[
            pl.BlockSpec(memory_space=pltpu.HBM),
            pl.BlockSpec(memory_space=pltpu.VMEM),
            pl.BlockSpec(memory_space=pltpu.VMEM),
            pl.BlockSpec(memory_space=pltpu.HBM),
            pl.BlockSpec(memory_space=pltpu.HBM),
            pl.BlockSpec(memory_space=pltpu.HBM),
        ],
        out_specs=pl.BlockSpec(memory_space=pltpu.VMEM),
        out_shape=jax.ShapeDtypeStruct((rows * 2 * blocks, LANES), jnp.int32),
        scratch_shapes=[
            pltpu.VMEM((ghost, rows, columns), jnp.bfloat16),
            pltpu.VMEM((slices, rows, columns), jnp.int32),
            pltpu.VMEM((ghost, PER, rows + 2 * SUB, LANES), jnp.float32),
            pltpu.VMEM((slices, rows, CB), jnp.float32),
            pltpu.VMEM((8, SUB, LANES), jnp.float32),
            pltpu.VMEM((CB + 2 * LANES, CB), jnp.bfloat16),
            pltpu.SMEM(color_table.shape, jnp.float32),
            pltpu.SMEM(extinction.shape, jnp.float32),
            pltpu.SemaphoreType.DMA((steps,)),
            pltpu.SemaphoreType.DMA((steps,)),
            pltpu.SemaphoreType.DMA((2,)),
        ],
        compiler_params=pltpu.CompilerParams(vmem_limit_bytes=61 << 20),
    )(density, low, high, material, color_table, extinction)


def blend_kernel(order_ref, part_ref, out_ref, place, image):
    bricks, rows, pairs, blocks, lanes = part_ref.shape
    for brick in range(bricks):
        place[order_ref[brick]] = brick
    spots = [(row, group) for row in range(rows) for group in range(0, blocks, SUB)]

    def walk(rank, carry):
        brick = place[rank]
        after = []
        for (row, group), (front, red, green, blue) in zip(spots, carry):
            first = part_ref[brick, row, 0, group : group + SUB, :]
            second = part_ref[brick, row, 1, group : group + SUB, :]
            low = LOG_LOW - front

            def seen(code):
                return jnp.exp2(code.astype(jnp.float32) * LOG_STEP + low)

            red = red + seen(lax.shift_right_logical(first, 16))
            green = green + seen(first & 0xFFFF)
            blue = blue + seen(lax.shift_right_logical(second, 16))
            front = front + (second & 0xFFFF).astype(jnp.float32) * TAU_STEP
            after.append((front, red, green, blue))
        return tuple(after)

    zero = jnp.zeros((SUB, lanes), jnp.float32)
    sums = lax.fori_loop(0, bricks, walk, tuple((zero,) * 4 for _ in spots), unroll=2)
    for (row, group), (front, red, green, blue) in zip(spots, sums):
        for channel, value in enumerate((red, green, blue, 1.0 - jnp.exp2(-front))):
            image[pl.ds((row * 4 + channel) * blocks + group, SUB), :] = value
    for row in range(rows):
        for block in range(blocks):
            out_ref[row, :, pl.ds(block * lanes, lanes)] = image[pl.ds(row * 4 * blocks + block, 4, stride=blocks), :]


def blend(order, part):
    bricks, rows, pairs, blocks, lanes = part.shape
    return pl.pallas_call(
        blend_kernel,
        in_specs=[pl.BlockSpec(memory_space=pltpu.SMEM), pl.BlockSpec(memory_space=pltpu.VMEM)],
        out_specs=pl.BlockSpec(memory_space=pltpu.VMEM),
        out_shape=jax.ShapeDtypeStruct((rows, 4, blocks * lanes), jnp.float32),
        scratch_shapes=[pltpu.SMEM((bricks,), jnp.int32), pltpu.VMEM((rows * 4 * blocks, lanes), jnp.float32)],
        compiler_params=pltpu.CompilerParams(vmem_limit_bytes=8 << 20),
    )(order, part)


def body(density, material, order, color_table, extinction):
    count = lax.axis_size("screen")
    rows, columns = density.shape[1], density.shape[2]
    bricks = lax.axis_size("depth")
    forward = [(i, i + 1) for i in range(count - 1)]
    backward = [(target, source) for source, target in forward]
    low = lax.ppermute(density[:, rows - 1 :], "screen", forward)
    high = lax.ppermute(density[:, :1], "screen", backward)
    coded = shade_bricks(density, low, high, material, color_table.T, extinction)
    blocks = columns // LANES
    strip = rows // bricks
    parts = coded.reshape(bricks, strip * 2 * blocks, LANES)
    parts = lax.all_to_all(parts, "depth", split_axis=0, concat_axis=0, tiled=True)
    image = blend(order, parts.reshape(bricks, strip, 2, blocks, LANES))
    return image.transpose(1, 0, 2)


def solution(mesh):
    placed = (P("depth", "screen", None), P("depth", "screen", None), P(), P(), P())
    return jax.shard_map(
        body,
        mesh=mesh,
        in_specs=placed,
        out_specs=P(None, ("screen", "depth"), None),
        check_vma=False,
    )
```

time: 66.1 us -> 59.6 us (0.902)
  Pallas kernels: 23.6 us -> 17.5 us
  other arithmetic: 2.61 us -> 0 us
  waiting for transfers between devices: 0.01 us -> 1.45 us
    pallas_call x1, Pallas kernels: 20.3 us -> 15.4 us  [shade_bricks(): pl.pallas_call(shade_kernel, in_specs=[pl.BlockSpec(memory_space=pltpu.HB...]
    ppermute x1, waiting for transfers between devices: 0.01 us -> 1.44 us  [body(): low = lax.ppermute(density[:, rows - 1:], 'screen', forward)]
    pallas_call x1, Pallas kernels: 3.33 us -> 2.04 us  [blend(): pl.pallas_call(blend_kernel, in_specs=[pl.BlockSpec(memory_space=pltpu.SM...]
    another operation x2 -> x0, other arithmetic: 1.24 us -> none  [the longest x1 0.97 us: band_matrices(): return jnp.stack([first, inner, last]).astype(jnp.bfloat16)]
    broadcast_in_dim x2 -> x0, local copies, waits for them, and re-layouts: 0.76 us -> none  [body(): tables = jnp.broadcast_to(entries.reshape(8, SUB, 1), (8, SUB, LANES))]
    concatenate x1 -> x0, other arithmetic: 0.69 us -> none  [body(): jnp.concatenate([(LOG2E * extinction)[None], color_table.T], axis=0)]
  transfers between devices with their start and end apart: 2 -> 2, of which waited for: 0 -> 1; matrix products, arithmetic and copies ran while one was open for 4% -> 0% of each run, Pallas kernels for 0% -> 0%
where the time goes in v2:
time: 59.6 us; the launch traced here: 58.9 us
  blocking collectives  31.4 us (53%)
  Pallas kernels  17.5 us (29%)
  starting transfers between devices  6.68 us (11%)
  local copies, waits for them, and re-layouts  1.84 us (3%)
  waiting for transfers between devices  1.45 us (2%)
    all_to_all x1, blocking collectives, body(): lax.all_to_all(parts, 'depth', split_axis=0, concat_axis=0, tiled=True)  31.4 us
    pallas_call x1, Pallas kernels, shade_bricks(): pl.pallas_call(shade_kernel, in_specs=[pl.BlockSpec(memory_space=pltpu.HB...  15.4 us
    ppermute x1, starting transfers between devices, body(): low = lax.ppermute(density[:, rows - 1:], 'screen', forward)  4.76 us
    pallas_call x1, Pallas kernels, blend(): pl.pallas_call(blend_kernel, in_specs=[pl.BlockSpec(memory_space=pltpu.SM...  2.04 us
    ppermute x1, starting transfers between devices, body(): high = lax.ppermute(density[:, :1], 'screen', backward)  1.92 us
    ppermute x1, waiting for transfers between devices, body(): low = lax.ppermute(density[:, rows - 1:], 'screen', forward)  1.44 us
    slice x1, local copies, waits for them, and re-layouts, body(): high = lax.ppermute(density[:, :1], 'screen', backward)  1.2 us
  transfers between devices with their start and end apart: 2, of which 1 were waited for; matrix products, arithmetic and copies ran while one was open for 0% of the time, Pallas kernels for 0%

profile of v2, /device:TPU:97, one launch (start us, length us, event | category | flops | bytes accessed | tf_op | source)
XLA Modules:
  0.0 58.9 jit_solution(12364307931343479394)
XLA Ops:
  0.0 1.2 %fusion = (bf16[10,1,2048]{2,1,0:T(2,128)(2,1)S(1)}, bf16[10,1,2048]{2,1,0:T(2,128)(2,1)S(1)}) fusion(bf16[10,96,2048]{2,1,0:T(8,128)(2,1)} %den_hbm.1), kind=kLoop, calls=%fused_computation | loop fusion | bytes 163840 | tf_op jit(solution)/shard_map/slice | solution.py:289
  1.2 1.9 %collective-permute-start.1 = (bf16[10,1,2048]{2,1,0:T(2,128)(2,1)S(1)}, bf16[10,1,2048]{2,1,0:T(2,128)(2,1)S(1)}, u32[]{:S(2)}, u32[]{:S(2)}) collective-permute-start(bf16[10,1,2048]{2,1,0:T(2,128)(2,1)S(1)} %get-tuple-element.5), channel_id=1, source_target_pairs={{1,0},{2,1},{3,2},{4,3},{5,4},{6,5},{7,6},{9,8},{10,9},{11,10},{12... | collective-permute-start | bytes 122888 | tf_op jit(solution)/shard_map/ppermute | solution.py:289
  3.1 4.8 %collective-permute-start = (bf16[10,1,2048]{2,1,0:T(2,128)(2,1)S(1)}, bf16[10,1,2048]{2,1,0:T(2,128)(2,1)S(1)}, u32[]{:S(2)}, u32[]{:S(2)}) collective-permute-start(bf16[10,1,2048]{2,1,0:T(2,128)(2,1)S(1)} %get-tuple-element.6), channel_id=1, source_target_pairs={{0,1},{1,2},{2,3},{3,4},{4,5},{5,6},{6,7},{8,9},{9,10},{10,11},{11... | collective-permute-start | bytes 122888 | tf_op jit(solution)/shard_map/ppermute | solution.py:288
  7.9 0.0 collective-permute-done.1.high_ref
  7.9 0.0 copy-start.1
  7.9 1.4 %collective-permute-done.low_ref = bf16[10,1,2048]{2,1,0:T(2,128)(2,1)S(1)} collective-permute-done((bf16[10,1,2048]{2,1,0:T(2,128)(2,1)S(1)}, bf16[10,1,2048]{2,1,0:T(2,128)(2,1)S(1)}, u32[]{:S(2)}, u32[]{:S(2)}) %collective-permute-start) | collective-permute-done | bytes 40992 | tf_op jit(solution)/shard_map/ppermute | solution.py:288
  9.4 0.0 copy-start.2
  9.4 0.0 copy-done.1
  9.4 0.6 %copy-done.2 = bf16[10,1,2048]{2,1,0:T(2,128)(2,1)} copy-done((bf16[10,1,2048]{2,1,0:T(2,128)(2,1)}, bf16[10,1,2048]{2,1,0:T(2,128)(2,1)S(1)}, u32[]{:S(2)}) %copy-start.2) | copy-done | bytes 40984
  10.0 0.0 copy-start
  10.0 15.4 %shard_map.55 = s32[3072,128]{1,0:T(8,128)} custom-call(bf16[10,96,2048]{2,1,0:T(8,128)(2,1)} %den_hbm.1, bf16[10,1,2048]{2,1,0:T(2,128)(2,1)} %copy-done.2, bf16[10,1,2048]{2,1,0:T(2,128)(2,1)} %copy-done.1, s32[8,96,2048]{2,1,0:T(8,128)} %mat_hbm.1, f32[3,16]{1,0:T(4,128)} %bitcast.6, f32[16]{0:T(128)} %ext_hbm.1), custom_call_target="tpu_custom_call" | custom-call | tf_op jit(solution)/shard_map/pallas_call | solution.py:207
  25.4 31.4 %all_to_all.5 = s32[32,96,128]{2,1,0:T(8,128)S(1)} all-to-all(s32[32,96,128]{2,1,0:T(8,128)} %bitcast.5), channel_id=1, replica_groups=mesh['depth'=32,'screen'=8] {'depth'}, dimensions={0} | all-to-all | bytes 3145728 | tf_op jit(solution)/shard_map/all_to_all | solution.py:294
  56.8 0.0 copy-done
  56.8 2.0 %shard_map.56 = f32[3,4,2048]{2,1,0:T(4,128)} custom-call(s32[32]{0:T(128)S(1)} %copy-done, s32[32,3,2,16,128]{4,3,2,1,0:T(8,128)S(1)} %bitcast.4), custom_call_target="tpu_custom_call" | custom-call | tf_op jit(solution)/shard_map/pallas_call | solution.py:272
Async XLA Ops:
  1.2 6.7 %collective-permute-start.1 = (bf16[10,1,2048]{2,1,0:T(2,128)(2,1)S(1)}, bf16[10,1,2048]{2,1,0:T(2,128)(2,1)S(1)}, u32[]{:S(2)}, u32[]{:S(2)}) collective-permute-start(bf16[10,1,2048]{2,1,0:T(2,128)(2,1)S(1)} %get-tuple-element.5), channel_id=1, source_target_pairs={{1,0},{2,1},{3,2},{4,3},{5,4},{6,5},{7,6},{9,8},{10,9},{11,10},{12... | collective-permute-start | bytes 122888 | tf_op jit(solution)/shard_map/ppermute | solution.py:289
  3.1 6.2 %collective-permute-start = (bf16[10,1,2048]{2,1,0:T(2,128)(2,1)S(1)}, bf16[10,1,2048]{2,1,0:T(2,128)(2,1)S(1)}, u32[]{:S(2)}, u32[]{:S(2)}) collective-permute-start(bf16[10,1,2048]{2,1,0:T(2,128)(2,1)S(1)} %get-tuple-element.6), channel_id=1, source_target_pairs={{0,1},{1,2},{2,3},{3,4},{4,5},{5,6},{6,7},{8,9},{9,10},{10,11},{11... | collective-permute-start | bytes 122888 | tf_op jit(solution)/shard_map/ppermute | solution.py:288
  7.9 1.5 %copy-start.1 = (bf16[10,1,2048]{2,1,0:T(2,128)(2,1)}, bf16[10,1,2048]{2,1,0:T(2,128)(2,1)S(1)}, u32[]{:S(2)}) copy-start(bf16[10,1,2048]{2,1,0:T(2,128)(2,1)S(1)} %collective-permute-done.1.high_ref) | copy-start | bytes 122884
  9.4 0.6 %copy-start.2 = (bf16[10,1,2048]{2,1,0:T(2,128)(2,1)}, bf16[10,1,2048]{2,1,0:T(2,128)(2,1)S(1)}, u32[]{:S(2)}) copy-start(bf16[10,1,2048]{2,1,0:T(2,128)(2,1)S(1)} %collective-permute-done.low_ref) | copy-start | bytes 122884
  10.0 46.8 %copy-start = (s32[32]{0:T(128)S(1)}, s32[32]{0:T(128)}, u32[]{:S(2)}) copy-start(s32[32]{0:T(128)} %order_ref.1) | copy-start | bytes 388

commit v3 on v2

--- a/solution.py
+++ b/solution.py
@@ -19,7 +19,8 @@
 CB = 256
 PER = CB // LANES
 CHUNK = 32
-LANE_TABLES = 1
+VLIM = 52
+LANE_TABLES = 2
 LOG2E = math.log2(math.e)
 
 SLICES = 8
@@ -85,11 +86,9 @@
     color_copy.start()
     ext_copy.start()
     den_copy(0).start()
+    mat_copy(0).start()
     den_copy(1).start()
-    for j in range(steps):
-        mat_copy(j).start()
-        if j + 2 < steps:
-            den_copy(j + 2).start()
+    mat_copy(1).start()
 
     source = lax.broadcasted_iota(jnp.int32, (2 * SUB, LANES), 0)
     target = lax.broadcasted_iota(jnp.int32, (2 * SUB, LANES), 1)
@@ -104,14 +103,14 @@
     for channel in range(LANE_TABLES):
         spread = jnp.zeros((SUB, LANES), jnp.float32)
         for entry in range(2 * SUB):
-            spread = jnp.where(lane == entry, (diffuse * light_x) * color_ref[channel, entry], spread)
+            spread = jnp.where(lane == entry, color_ref[channel, entry], spread)
         table[2 + 2 * channel] = spread
     for entry in range(SUB):
         for half in range(2):
             spot = entry + half * SUB
-            table[half, entry : entry + 1, :] = jnp.full((1, LANES), -LOG2E * ext_ref[spot], jnp.float32)
+            table[half, entry : entry + 1, :] = jnp.full((1, LANES), ext_ref[spot], jnp.float32)
             for channel in range(LANE_TABLES, 3):
-                scale = (diffuse * light_x) * color_ref[channel, spot]
+                scale = color_ref[channel, spot]
                 table[2 + 2 * channel + half, entry : entry + 1, :] = jnp.full((1, LANES), scale, jnp.float32)
     tables = [table[i] for i in range(8)]
 
@@ -121,6 +120,12 @@
             den_copy(j + 1).wait()
 
         mat_copy(j).wait()
+
+        @pl.when(j + 2 < steps)
+        def _():
+            den_copy(j + 2).start()
+            mat_copy(j + 2).start()
+
         start = pl.multiple_of(j * CB, CB)
         left = pl.multiple_of(jnp.maximum(start - LANES, 0), LANES)
         right = pl.multiple_of(jnp.minimum(start + CB, columns - LANES), LANES)
@@ -229,8 +234,8 @@
             pltpu.SemaphoreType.DMA((steps,)),
             pltpu.SemaphoreType.DMA((2,)),
         ],
-        compiler_params=pltpu.CompilerParams(vmem_limit_bytes=61 << 20),
-    )(density, low, high, material, color_table, extinction)
+        compiler_params=pltpu.CompilerParams(vmem_limit_bytes=VLIM << 20),
+    )(density, low, high, material, (diffuse * light_x) * color_table, -LOG2E * extinction)
 
 
 def blend_kernel(order_ref, part_ref, out_ref, place, image):
@@ -258,7 +263,7 @@
         return tuple(after)
 
     zero = jnp.zeros((SUB, lanes), jnp.float32)
-    sums = lax.fori_loop(0, bricks, walk, tuple((zero,) * 4 for _ in spots), unroll=2)
+    sums = lax.fori_loop(0, bricks, walk, tuple((zero,) * 4 for _ in spots), unroll=4)
     for (row, group), (front, red, green, blue) in zip(spots, sums):
         for channel, value in enumerate((red, green, blue, 1.0 - jnp.exp2(-front))):
             image[pl.ds((row * 4 + channel) * blocks + group, SUB), :] = value

time: 59.6 us -> 56.4 us (0.946)
  Pallas kernels: 17.5 us -> 15.2 us
  other arithmetic: 0 us -> 1.34 us
  waiting for transfers between devices: 1.45 us -> 0.12 us
  local copies, waits for them, and re-layouts: 1.84 us -> 1.21 us
    pallas_call x1, Pallas kernels: 15.4 us -> 13.2 us  [shade_bricks(): pl.pallas_call(shade_kernel, in_specs=[pl.BlockSpec(memory_space=pltpu.HB...]
    mul x0 -> x2, other arithmetic: none -> 1.34 us  [the longest x1 0.69 us: shade_bricks(): diffuse * light_x * color_table]
    ppermute x1, waiting for transfers between devices: 1.44 us -> 0.11 us  [body(): low = lax.ppermute(density[:, rows - 1:], 'screen', forward)]
    unnamed x6 -> x2, local copies, waits for them, and re-layouts: 0.64 us -> 0.01 us
  transfers between devices with their start and end apart: 2 -> 2, of which waited for: 1 -> 1; matrix products, arithmetic and copies ran while one was open for 0% -> 2% of each run, Pallas kernels for 0% -> 0%
where the time goes in v3:
time: 56.4 us; the launch traced here: 55.7 us
  blocking collectives  31.2 us (55%)
  Pallas kernels  15.2 us (27%)
  starting transfers between devices  6.68 us (12%)
  other arithmetic  1.34 us (2%)
  local copies, waits for them, and re-layouts  1.21 us (2%)
    all_to_all x1, blocking collectives, body(): lax.all_to_all(parts, 'depth', split_axis=0, concat_axis=0, tiled=True)  31.2 us
    pallas_call x1, Pallas kernels, shade_bricks(): pl.pallas_call(shade_kernel, in_specs=[pl.BlockSpec(memory_space=pltpu.HB...  13.2 us
    ppermute x1, starting transfers between devices, body(): low = lax.ppermute(density[:, rows - 1:], 'screen', forward)  4.76 us
    pallas_call x1, Pallas kernels, blend(): pl.pallas_call(blend_kernel, in_specs=[pl.BlockSpec(memory_space=pltpu.SM...  1.93 us
    ppermute x1, starting transfers between devices, body(): high = lax.ppermute(density[:, :1], 'screen', backward)  1.92 us
    slice x1, local copies, waits for them, and re-layouts, body(): high = lax.ppermute(density[:, :1], 'screen', backward)  1.2 us
  transfers between devices with their start and end apart: 2, of which 1 were waited for; matrix products, arithmetic and copies ran while one was open for 2% of the time, Pallas kernels for 0%

profile of v3, /device:TPU:97, one launch (start us, length us, event | category | flops | bytes accessed | tf_op | source)
XLA Modules:
  0.0 55.7 jit_solution(12446713422904425476)
XLA Ops:
  0.0 1.2 %fusion = (bf16[10,1,2048]{2,1,0:T(2,128)(2,1)S(1)}, bf16[10,1,2048]{2,1,0:T(2,128)(2,1)S(1)}) fusion(bf16[10,96,2048]{2,1,0:T(8,128)(2,1)} %den_hbm.1), kind=kLoop, calls=%fused_computation.2 | loop fusion | bytes 163840 | tf_op jit(solution)/shard_map/slice | solution.py:294
  1.2 1.9 %collective-permute-start.1 = (bf16[10,1,2048]{2,1,0:T(2,128)(2,1)S(1)}, bf16[10,1,2048]{2,1,0:T(2,128)(2,1)S(1)}, u32[]{:S(2)}, u32[]{:S(2)}) collective-permute-start(bf16[10,1,2048]{2,1,0:T(2,128)(2,1)S(1)} %get-tuple-element.5), channel_id=1, source_target_pairs={{1,0},{2,1},{3,2},{4,3},{5,4},{6,5},{7,6},{9,8},{10,9},{11,10},{12... | collective-permute-start | bytes 122888 | tf_op jit(solution)/shard_map/ppermute | solution.py:294
  3.1 4.8 %collective-permute-start = (bf16[10,1,2048]{2,1,0:T(2,128)(2,1)S(1)}, bf16[10,1,2048]{2,1,0:T(2,128)(2,1)S(1)}, u32[]{:S(2)}, u32[]{:S(2)}) collective-permute-start(bf16[10,1,2048]{2,1,0:T(2,128)(2,1)S(1)} %get-tuple-element.6), channel_id=1, source_target_pairs={{0,1},{1,2},{2,3},{3,4},{4,5},{5,6},{6,7},{8,9},{9,10},{10,11},{11... | collective-permute-start | bytes 122888 | tf_op jit(solution)/shard_map/ppermute | solution.py:293
  7.9 0.7 %multiply_bitcast_fusion.color_hbm = f32[3,16]{1,0:T(4,128)S(1)} fusion(f32[16,3]{0,1:T(4,128)} %param.8), kind=kLoop, calls=%fused_computation | loop fusion | flops 48 | bytes 384 | tf_op jit(solution)/shard_map/mul | solution.py:238
  8.6 0.7 %broadcast_multiply_fusion.ext_hbm = f32[16]{0:T(128)S(1)} fusion(f32[16]{0:T(128)} %param.9), kind=kLoop, calls=%fused_computation.1 | loop fusion | flops 16 | bytes 128 | tf_op jit(solution)/shard_map/mul | solution.py:238
  9.2 0.0 copy-start
  9.2 0.0 collective-permute-done.1.high_ref
  9.2 0.1 collective-permute-done.low_ref
  9.4 13.2 %shard_map.55 = s32[3072,128]{1,0:T(8,128)S(1)} custom-call(bf16[10,96,2048]{2,1,0:T(8,128)(2,1)} %den_hbm.1, bf16[10,1,2048]{2,1,0:T(2,128)(2,1)S(1)} %collective-permute-done.low_ref, bf16[10,1,2048]{2,1,0:T(2,128)(2,1)S(1)} %collective-permute-done.1.high_ref, s32[8,96,2048]{2,1,0:T(8,128)} %mat_hbm.1, f32[3,16]{1,0:T(4,128)S(1)} %multiply_bitcast_fusion.color_hbm, ...), custom_call_target="tpu_custom_call" | custom-call | tf_op jit(solution)/shard_map/pallas_call | solution.py:212
  22.6 31.2 %all_to_all.5 = s32[32,96,128]{2,1,0:T(8,128)S(1)} all-to-all(s32[32,96,128]{2,1,0:T(8,128)S(1)} %bitcast.5), channel_id=1, replica_groups=mesh['depth'=32,'screen'=8] {'depth'}, dimensions={0} | all-to-all | bytes 3145728 | tf_op jit(solution)/shard_map/all_to_all | solution.py:299
  53.8 0.0 copy-done
  53.8 1.9 %shard_map.56 = f32[3,4,2048]{2,1,0:T(4,128)} custom-call(s32[32]{0:T(128)S(1)} %copy-done, s32[32,3,2,16,128]{4,3,2,1,0:T(8,128)S(1)} %bitcast.6), custom_call_target="tpu_custom_call" | custom-call | tf_op jit(solution)/shard_map/pallas_call | solution.py:277
Async XLA Ops:
  1.2 8.0 %collective-permute-start.1 = (bf16[10,1,2048]{2,1,0:T(2,128)(2,1)S(1)}, bf16[10,1,2048]{2,1,0:T(2,128)(2,1)S(1)}, u32[]{:S(2)}, u32[]{:S(2)}) collective-permute-start(bf16[10,1,2048]{2,1,0:T(2,128)(2,1)S(1)} %get-tuple-element.5), channel_id=1, source_target_pairs={{1,0},{2,1},{3,2},{4,3},{5,4},{6,5},{7,6},{9,8},{10,9},{11,10},{12... | collective-permute-start | bytes 122888 | tf_op jit(solution)/shard_map/ppermute | solution.py:294
  3.1 6.2 %collective-permute-start = (bf16[10,1,2048]{2,1,0:T(2,128)(2,1)S(1)}, bf16[10,1,2048]{2,1,0:T(2,128)(2,1)S(1)}, u32[]{:S(2)}, u32[]{:S(2)}) collective-permute-start(bf16[10,1,2048]{2,1,0:T(2,128)(2,1)S(1)} %get-tuple-element.6), channel_id=1, source_target_pairs={{0,1},{1,2},{2,3},{3,4},{4,5},{5,6},{6,7},{8,9},{9,10},{10,11},{11... | collective-permute-start | bytes 122888 | tf_op jit(solution)/shard_map/ppermute | solution.py:293
  9.2 44.5 %copy-start = (s32[32]{0:T(128)S(1)}, s32[32]{0:T(128)}, u32[]{:S(2)}) copy-start(s32[32]{0:T(128)} %order_ref.1) | copy-start | bytes 388

commit v4 on v3

--- a/solution.py
+++ b/solution.py
@@ -66,30 +66,7 @@
     return jnp.where(upper, entries_at(high_table, index), entries_at(low_table, index))
 
 
-def shade_kernel(den_hbm, low_ref, high_ref, mat_hbm, color_hbm, ext_hbm, out_ref, den, mat, full, diff, table, band, color_ref, ext_ref, den_sem, mat_sem, table_sem):
-    ghost, rows, columns = den.shape
-    slices = ghost - 2
-    steps = columns // CB
-    blocks = columns // LANES
-    stride = 2 * blocks
-
-    def den_copy(j):
-        cols = pl.ds(pl.multiple_of(j * CB, CB), CB)
-        return pltpu.make_async_copy(den_hbm.at[:, :, cols], den.at[:, :, cols], den_sem.at[j])
-
-    def mat_copy(j):
-        cols = pl.ds(pl.multiple_of(j * CB, CB), CB)
-        return pltpu.make_async_copy(mat_hbm.at[:, :, cols], mat.at[:, :, cols], mat_sem.at[j])
-
-    color_copy = pltpu.make_async_copy(color_hbm, color_ref, table_sem.at[0])
-    ext_copy = pltpu.make_async_copy(ext_hbm, ext_ref, table_sem.at[1])
-    color_copy.start()
-    ext_copy.start()
-    den_copy(0).start()
-    mat_copy(0).start()
-    den_copy(1).start()
-    mat_copy(1).start()
-
+def prepare_kernel(color_ref, ext_ref, table, band):
     source = lax.broadcasted_iota(jnp.int32, (2 * SUB, LANES), 0)
     target = lax.broadcasted_iota(jnp.int32, (2 * SUB, LANES), 1)
     for top in range(0, CB + 2 * LANES, 2 * SUB):
@@ -97,21 +74,57 @@
             shift = (source + (top - LANES)) - (target + side)
             tile = (shift == 1).astype(jnp.float32) - (shift == -1).astype(jnp.float32)
             band[top : top + 2 * SUB, side : side + LANES] = tile.astype(jnp.bfloat16)
-    color_copy.wait()
-    ext_copy.wait()
     lane = lax.broadcasted_iota(jnp.int32, (SUB, LANES), 1)
     for channel in range(LANE_TABLES):
+        table[3 + 2 * channel] = jnp.zeros((SUB, LANES), jnp.float32)
         spread = jnp.zeros((SUB, LANES), jnp.float32)
         for entry in range(2 * SUB):
-            spread = jnp.where(lane == entry, color_ref[channel, entry], spread)
+            spread = jnp.where(lane == entry, (diffuse * light_x) * color_ref[channel, entry], spread)
         table[2 + 2 * channel] = spread
     for entry in range(SUB):
         for half in range(2):
             spot = entry + half * SUB
-            table[half, entry : entry + 1, :] = jnp.full((1, LANES), ext_ref[spot], jnp.float32)
+            table[half, entry : entry + 1, :] = jnp.full((1, LANES), -LOG2E * ext_ref[spot], jnp.float32)
             for channel in range(LANE_TABLES, 3):
-                scale = color_ref[channel, spot]
+                scale = (diffuse * light_x) * color_ref[channel, spot]
                 table[2 + 2 * channel + half, entry : entry + 1, :] = jnp.full((1, LANES), scale, jnp.float32)
+
+
+def prepare(color_table, extinction):
+    smem = pl.BlockSpec(memory_space=pltpu.SMEM)
+    vmem = pl.BlockSpec(memory_space=pltpu.VMEM)
+    return pl.pallas_call(
+        prepare_kernel,
+        in_specs=[smem, smem],
+        out_specs=[vmem, vmem],
+        out_shape=[
+            jax.ShapeDtypeStruct((8, SUB, LANES), jnp.float32),
+            jax.ShapeDtypeStruct((CB + 2 * LANES, CB), jnp.bfloat16),
+        ],
+        compiler_params=pltpu.CompilerParams(vmem_limit_bytes=VLIM << 20),
+    )(color_table, extinction)
+
+
+def shade_kernel(den_hbm, low_ref, high_ref, mat_hbm, table, band, out_ref, den, mat, full, diff, den_sem, mat_sem):
+    ghost, rows, columns = den.shape
+    slices = ghost - 2
+    steps = columns // CB
+    blocks = columns // LANES
+    stride = 2 * blocks
+
+    def den_copy(j):
+        cols = pl.ds(pl.multiple_of(j * CB, CB), CB)
+        return pltpu.make_async_copy(den_hbm.at[:, :, cols], den.at[:, :, cols], den_sem.at[j])
+
+    def mat_copy(j):
+        cols = pl.ds(pl.multiple_of(j * CB, CB), CB)
+        return pltpu.make_async_copy(mat_hbm.at[:, :, cols], mat.at[:, :, cols], mat_sem.at[j])
+
+    den_copy(0).start()
+    mat_copy(0).start()
+    den_copy(1).start()
+    mat_copy(1).start()
+
     tables = [table[i] for i in range(8)]
 
     def shade_columns(j, carry):
@@ -136,11 +149,11 @@
             for z in range(ghost):
                 for c in range(PER):
                     cols = pl.ds(start + c * LANES, LANES)
-                    if r == 0:
-                        full[z, c, SUB - 1 : SUB, :] = low_ref[z, :, cols].astype(jnp.float32)
+                    if r == 0 and 0 < z < ghost - 1:
+                        full[z, c, SUB - 1 : SUB, :] = low_ref[z - 1 : z, cols].astype(jnp.float32)
                     full[z, c, pl.ds(SUB + r * CHUNK, CHUNK), :] = den[z, pl.ds(r * CHUNK, CHUNK), cols].astype(jnp.float32)
-                    if r == rows // CHUNK - 1:
-                        full[z, c, SUB + rows : SUB + rows + 1, :] = high_ref[z, :, cols].astype(jnp.float32)
+                    if r == rows // CHUNK - 1 and 0 < z < ghost - 1:
+                        full[z, c, SUB + rows : SUB + rows + 1, :] = high_ref[z - 1 : z, cols].astype(jnp.float32)
 
         def across(r):
             spots = pl.ds(r * CHUNK, CHUNK)
@@ -205,6 +218,7 @@
 
 
 def shade_bricks(density, low, high, material, color_table, extinction):
+    table, band = prepare(color_table, extinction)
     ghost, rows, columns = density.shape
     slices = material.shape[0]
     steps = columns // CB
@@ -216,8 +230,8 @@
             pl.BlockSpec(memory_space=pltpu.VMEM),
             pl.BlockSpec(memory_space=pltpu.VMEM),
             pl.BlockSpec(memory_space=pltpu.HBM),
-            pl.BlockSpec(memory_space=pltpu.HBM),
-            pl.BlockSpec(memory_space=pltpu.HBM),
+            pl.BlockSpec(memory_space=pltpu.VMEM),
+            pl.BlockSpec(memory_space=pltpu.VMEM),
         ],
         out_specs=pl.BlockSpec(memory_space=pltpu.VMEM),
         out_shape=jax.ShapeDtypeStruct((rows * 2 * blocks, LANES), jnp.int32),
@@ -226,16 +240,42 @@
             pltpu.VMEM((slices, rows, columns), jnp.int32),
             pltpu.VMEM((ghost, PER, rows + 2 * SUB, LANES), jnp.float32),
             pltpu.VMEM((slices, rows, CB), jnp.float32),
-            pltpu.VMEM((8, SUB, LANES), jnp.float32),
-            pltpu.VMEM((CB + 2 * LANES, CB), jnp.bfloat16),
-            pltpu.SMEM(color_table.shape, jnp.float32),
-            pltpu.SMEM(extinction.shape, jnp.float32),
             pltpu.SemaphoreType.DMA((steps,)),
             pltpu.SemaphoreType.DMA((steps,)),
-            pltpu.SemaphoreType.DMA((2,)),
         ],
         compiler_params=pltpu.CompilerParams(vmem_limit_bytes=VLIM << 20),
-    )(density, low, high, material, (diffuse * light_x) * color_table, -LOG2E * extinction)
+    )(density, low, high, material, table, band)
+
+
+def end_rows_kernel(den_hbm, first_ref, last_ref, top, bottom, sem):
+    slices, tile = top.shape[0], top.shape[1]
+    rows = den_hbm.shape[1]
+    copies = [
+        pltpu.make_async_copy(den_hbm.at[1 : 1 + slices, start : start + tile, :], held, sem.at[i])
+        for i, (start, held) in enumerate(((0, top), (rows - tile, bottom)))
+    ]
+    for copy in copies:
+        copy.start()
+    for copy in copies:
+        copy.wait()
+    for z in range(slices):
+        first_ref[z : z + 1, :] = top[z, :1, :]
+        last_ref[z : z + 1, :] = bottom[z, tile - 1 :, :]
+
+
+def end_rows(density):
+    ghost, rows, columns = density.shape
+    row = jax.ShapeDtypeStruct((ghost - 2, columns), density.dtype)
+    vmem = pl.BlockSpec(memory_space=pltpu.VMEM)
+    tile = pltpu.VMEM((ghost - 2, SUB, columns), density.dtype)
+    return pl.pallas_call(
+        end_rows_kernel,
+        in_specs=[pl.BlockSpec(memory_space=pltpu.HBM)],
+        out_specs=[vmem, vmem],
+        out_shape=[row, row],
+        scratch_shapes=[tile, tile, pltpu.SemaphoreType.DMA((2,))],
+        compiler_params=pltpu.CompilerParams(vmem_limit_bytes=VLIM << 20),
+    )(density)
 
 
 def blend_kernel(order_ref, part_ref, out_ref, place, image):
@@ -263,7 +303,7 @@
         return tuple(after)
 
     zero = jnp.zeros((SUB, lanes), jnp.float32)
-    sums = lax.fori_loop(0, bricks, walk, tuple((zero,) * 4 for _ in spots), unroll=4)
+    sums = lax.fori_loop(0, bricks, walk, tuple((zero,) * 4 for _ in spots), unroll=16)
     for (row, group), (front, red, green, blue) in zip(spots, sums):
         for channel, value in enumerate((red, green, blue, 1.0 - jnp.exp2(-front))):
             image[pl.ds((row * 4 + channel) * blocks + group, SUB), :] = value
@@ -290,8 +330,9 @@
     bricks = lax.axis_size("depth")
     forward = [(i, i + 1) for i in range(count - 1)]
     backward = [(target, source) for source, target in forward]
-    low = lax.ppermute(density[:, rows - 1 :], "screen", forward)
-    high = lax.ppermute(density[:, :1], "screen", backward)
+    first, last = end_rows(density)
+    low = lax.ppermute(last, "screen", forward)
+    high = lax.ppermute(first, "screen", backward)
     coded = shade_bricks(density, low, high, material, color_table.T, extinction)
     blocks = columns // LANES
     strip = rows // bricks

time: 56.4 us -> 58.6 us (1.039)
  waiting for transfers between devices: 0.12 us -> 3.25 us
  Pallas kernels: 15.2 us -> 16.7 us
  other arithmetic: 1.34 us -> 0 us
  local copies, waits for them, and re-layouts: 1.21 us -> 0.01 us
    ppermute x2, waiting for transfers between devices: 0.12 us -> 3.25 us  [the longest x1 3.25 us: body(): high = lax.ppermute(first, 'screen', backward)]
    pallas_call x0 -> x2, Pallas kernels: none -> 1.81 us  [the longest x1 1.16 us: end_rows(): pl.pallas_call(end_rows_kernel, in_specs=[pl.BlockSpec(memory_space=pltpu...]
    mul x2 -> x0, other arithmetic: 1.34 us -> none  [the longest x1 0.69 us: shade_bricks(): diffuse * light_x * color_table]
    slice x1 -> x0, local copies, waits for them, and re-layouts: 1.2 us -> none  [body(): high = lax.ppermute(density[:, :1], 'screen', backward)]
  transfers between devices with their start and end apart: 2 -> 2, of which waited for: 1 -> 1; matrix products, arithmetic and copies ran while one was open for 2% -> 0% of each run, Pallas kernels for 0% -> 1%
where the time goes in v4:
time: 58.6 us; the launch traced here: 58.4 us
  blocking collectives  31.7 us (54%)
  Pallas kernels  16.7 us (28%)
  starting transfers between devices  6.68 us (11%)
  waiting for transfers between devices  3.25 us (6%)
    all_to_all x1, blocking collectives, body(): lax.all_to_all(parts, 'depth', split_axis=0, concat_axis=0, tiled=True)  31.7 us
    pallas_call x1, Pallas kernels, shade_bricks(): pl.pallas_call(shade_kernel, in_specs=[pl.BlockSpec(memory_space=pltpu.HB...  13 us
    ppermute x1, starting transfers between devices, body(): low = lax.ppermute(last, 'screen', forward)  4.76 us
    ppermute x1, waiting for transfers between devices, body(): high = lax.ppermute(first, 'screen', backward)  3.25 us
    ppermute x1, starting transfers between devices, body(): high = lax.ppermute(first, 'screen', backward)  1.92 us
    pallas_call x1, Pallas kernels, blend(): pl.pallas_call(blend_kernel, in_specs=[pl.BlockSpec(memory_space=pltpu.SM...  1.86 us
  transfers between devices with their start and end apart: 2, of which 1 were waited for; matrix products, arithmetic and copies ran while one was open for 0% of the time, Pallas kernels for 1%

profile of v4, /device:TPU:97, one launch (start us, length us, event | category | flops | bytes accessed | tf_op | source)
XLA Modules:
  0.0 58.4 jit_solution(7358833251903208400)
XLA Ops:
  0.0 0.0 copy-start.2
  0.0 0.0 copy-start
  0.0 1.2 %shard_map.55 = (bf16[8,2048]{1,0:T(8,128)(2,1)S(1)}, bf16[8,2048]{1,0:T(8,128)(2,1)S(1)}) custom-call(bf16[10,96,2048]{2,1,0:T(8,128)(2,1)} %den_hbm.3), custom_call_target="tpu_custom_call" | custom-call | tf_op jit(solution)/shard_map/pallas_call | solution.py:271
  1.2 4.8 %collective-permute-start = (bf16[8,2048]{1,0:T(8,128)(2,1)S(1)}, bf16[8,2048]{1,0:T(8,128)(2,1)S(1)}, u32[]{:S(2)}, u32[]{:S(2)}) collective-permute-start(bf16[8,2048]{1,0:T(8,128)(2,1)S(1)} %get-tuple-element.9), channel_id=1, source_target_pairs={{0,1},{1,2},{2,3},{3,4},{4,5},{5,6},{6,7},{8,9},{9,10},{10,11},{11... | collective-permute-start | bytes 98312 | tf_op jit(solution)/shard_map/ppermute | solution.py:334
  5.9 1.9 %collective-permute-start.1 = (bf16[8,2048]{1,0:T(8,128)(2,1)S(1)}, bf16[8,2048]{1,0:T(8,128)(2,1)S(1)}, u32[]{:S(2)}, u32[]{:S(2)}) collective-permute-start(bf16[8,2048]{1,0:T(8,128)(2,1)S(1)} %get-tuple-element.10), channel_id=1, source_target_pairs={{1,0},{2,1},{3,2},{4,3},{5,4},{6,5},{7,6},{9,8},{10,9},{11,10},{12... | collective-permute-start | bytes 98312 | tf_op jit(solution)/shard_map/ppermute | solution.py:335
  7.9 0.0 copy-done.2
  7.9 0.0 copy-done
  7.9 0.7 %shard_map.56 = (f32[8,8,128]{2,1,0:T(8,128)S(1)}, bf16[512,256]{1,0:T(8,128)(2,1)S(1)}) custom-call(f32[3,16]{1,0:T(4,128)S(1)} %bitcast.6, f32[16]{0:T(128)S(1)} %copy-done.2), custom_call_target="tpu_custom_call" | custom-call | tf_op jit(solution)/shard_map/pallas_call | solution.py:96
  8.5 0.0 collective-permute-done.low_ref
  8.6 3.2 %collective-permute-done.1.high_ref = bf16[8,2048]{1,0:T(8,128)(2,1)S(1)} collective-permute-done((bf16[8,2048]{1,0:T(8,128)(2,1)S(1)}, bf16[8,2048]{1,0:T(8,128)(2,1)S(1)}, u32[]{:S(2)}, u32[]{:S(2)}) %collective-permute-start.1) | collective-permute-done | bytes 32800 | tf_op jit(solution)/shard_map/ppermute | solution.py:335
  11.8 0.0 copy-start.1
  11.8 13.0 %shard_map.57 = s32[3072,128]{1,0:T(8,128)S(1)} custom-call(bf16[10,96,2048]{2,1,0:T(8,128)(2,1)} %den_hbm.3, bf16[8,2048]{1,0:T(8,128)(2,1)S(1)} %collective-permute-done.low_ref, bf16[8,2048]{1,0:T(8,128)(2,1)S(1)} %collective-permute-done.1.high_ref, s32[8,96,2048]{2,1,0:T(8,128)} %mat_hbm.1, f32[8,8,128]{2,1,0:T(8,128)S(1)} %get-tuple-element.11.table, ...), custom_call_target="tpu_custom_call" | custom-call | tf_op jit(solution)/shard_map/pallas_call | solution.py:226
  24.8 31.7 %all_to_all.5 = s32[32,96,128]{2,1,0:T(8,128)S(1)} all-to-all(s32[32,96,128]{2,1,0:T(8,128)S(1)} %bitcast.5), channel_id=1, replica_groups=mesh['depth'=32,'screen'=8] {'depth'}, dimensions={0} | all-to-all | bytes 3145728 | tf_op jit(solution)/shard_map/all_to_all | solution.py:340
  56.5 0.0 copy-done.1
  56.5 1.9 %shard_map.58 = f32[3,4,2048]{2,1,0:T(4,128)} custom-call(s32[32]{0:T(128)S(1)} %copy-done.1, s32[32,3,2,16,128]{4,3,2,1,0:T(8,128)S(1)} %bitcast.4), custom_call_target="tpu_custom_call" | custom-call | tf_op jit(solution)/shard_map/pallas_call | solution.py:317
Async XLA Ops:
  0.0 7.9 %copy-start.2 = (f32[16]{0:T(128)S(1)}, f32[16]{0:T(128)}, u32[]{:S(2)}) copy-start(f32[16]{0:T(128)} %ext_ref.1) | copy-start | bytes 196
  0.0 7.9 %copy-start = (f32[16,3]{0,1:T(4,128)S(1)}, f32[16,3]{0,1:T(4,128)}, u32[]{:S(2)}) copy-start(f32[16,3]{0,1:T(4,128)} %param.8) | copy-start | bytes 580
  1.2 7.4 %collective-permute-start = (bf16[8,2048]{1,0:T(8,128)(2,1)S(1)}, bf16[8,2048]{1,0:T(8,128)(2,1)S(1)}, u32[]{:S(2)}, u32[]{:S(2)}) collective-permute-start(bf16[8,2048]{1,0:T(8,128)(2,1)S(1)} %get-tuple-element.9), channel_id=1, source_target_pairs={{0,1},{1,2},{2,3},{3,4},{4,5},{5,6},{6,7},{8,9},{9,10},{10,11},{11... | collective-permute-start | bytes 98312 | tf_op jit(solution)/shard_map/ppermute | solution.py:334
  5.9 5.9 %collective-permute-start.1 = (bf16[8,2048]{1,0:T(8,128)(2,1)S(1)}, bf16[8,2048]{1,0:T(8,128)(2,1)S(1)}, u32[]{:S(2)}, u32[]{:S(2)}) collective-permute-start(bf16[8,2048]{1,0:T(8,128)(2,1)S(1)} %get-tuple-element.10), channel_id=1, source_target_pairs={{1,0},{2,1},{3,2},{4,3},{5,4},{6,5},{7,6},{9,8},{10,9},{11,10},{12... | collective-permute-start | bytes 98312 | tf_op jit(solution)/shard_map/ppermute | solution.py:335
  11.8 44.7 %copy-start.1 = (s32[32]{0:T(128)S(1)}, s32[32]{0:T(128)}, u32[]{:S(2)}) copy-start(s32[32]{0:T(128)} %order_ref.1) | copy-start | bytes 388

commit v5 on v4

--- a/solution.py
+++ b/solution.py
@@ -105,7 +105,7 @@
     )(color_table, extinction)
 
 
-def shade_kernel(den_hbm, low_ref, high_ref, mat_hbm, table, band, out_ref, den, mat, full, diff, den_sem, mat_sem):
+def shade_kernel(den_hbm, high_ref, low_ref, mat_hbm, table, band, out_ref, den, mat, full, diff, den_sem, mat_sem):
     ghost, rows, columns = den.shape
     slices = ghost - 2
     steps = columns // CB
@@ -244,7 +244,7 @@
             pltpu.SemaphoreType.DMA((steps,)),
         ],
         compiler_params=pltpu.CompilerParams(vmem_limit_bytes=VLIM << 20),
-    )(density, low, high, material, table, band)
+    )(density, high, low, material, table, band)
 
 
 def end_rows_kernel(den_hbm, first_ref, last_ref, top, bottom, sem):

time: 58.6 us -> 55.6 us (0.949)
  waiting for transfers between devices: 3.25 us -> 0.31 us
    ppermute x1, waiting for transfers between devices: 3.25 us -> 0.01 us  [body(): high = lax.ppermute(first, 'screen', backward)]
where the time goes in v5:
time: 55.6 us; the launch traced here: 54.9 us
  blocking collectives  31.2 us (56%)
  Pallas kernels  16.7 us (30%)
  starting transfers between devices  6.68 us (12%)
    all_to_all x1, blocking collectives, body(): lax.all_to_all(parts, 'depth', split_axis=0, concat_axis=0, tiled=True)  31.2 us
    pallas_call x1, Pallas kernels, shade_bricks(): pl.pallas_call(shade_kernel, in_specs=[pl.BlockSpec(memory_space=pltpu.HB...  13 us
    ppermute x1, starting transfers between devices, body(): low = lax.ppermute(last, 'screen', forward)  4.76 us
    ppermute x1, starting transfers between devices, body(): high = lax.ppermute(first, 'screen', backward)  1.92 us
    pallas_call x1, Pallas kernels, blend(): pl.pallas_call(blend_kernel, in_specs=[pl.BlockSpec(memory_space=pltpu.SM...  1.86 us
    pallas_call x1, Pallas kernels, end_rows(): pl.pallas_call(end_rows_kernel, in_specs=[pl.BlockSpec(memory_space=pltpu...  1.16 us
  transfers between devices with their start and end apart: 2, of which 1 were waited for; matrix products, arithmetic and copies ran while one was open for 0% of the time, Pallas kernels for 1%

profile of v5, /device:TPU:97, one launch (start us, length us, event | category | flops | bytes accessed | tf_op | source)
XLA Modules:
  0.0 54.9 jit_solution(2195932892302181407)
XLA Ops:
  0.0 0.0 copy-start.2
  0.0 0.0 copy-start
  0.0 1.2 %shard_map.55 = (bf16[8,2048]{1,0:T(8,128)(2,1)S(1)}, bf16[8,2048]{1,0:T(8,128)(2,1)S(1)}) custom-call(bf16[10,96,2048]{2,1,0:T(8,128)(2,1)} %den_hbm.3), custom_call_target="tpu_custom_call" | custom-call | tf_op jit(solution)/shard_map/pallas_call | solution.py:271
  1.2 1.9 %collective-permute-start = (bf16[8,2048]{1,0:T(8,128)(2,1)S(1)}, bf16[8,2048]{1,0:T(8,128)(2,1)S(1)}, u32[]{:S(2)}, u32[]{:S(2)}) collective-permute-start(bf16[8,2048]{1,0:T(8,128)(2,1)S(1)} %get-tuple-element.9), channel_id=1, source_target_pairs={{1,0},{2,1},{3,2},{4,3},{5,4},{6,5},{7,6},{9,8},{10,9},{11,10},{12... | collective-permute-start | bytes 98312 | tf_op jit(solution)/shard_map/ppermute | solution.py:335
  3.1 4.8 %collective-permute-start.1 = (bf16[8,2048]{1,0:T(8,128)(2,1)S(1)}, bf16[8,2048]{1,0:T(8,128)(2,1)S(1)}, u32[]{:S(2)}, u32[]{:S(2)}) collective-permute-start(bf16[8,2048]{1,0:T(8,128)(2,1)S(1)} %get-tuple-element.10), channel_id=1, source_target_pairs={{0,1},{1,2},{2,3},{3,4},{4,5},{5,6},{6,7},{8,9},{9,10},{10,11},{11... | collective-permute-start | bytes 98312 | tf_op jit(solution)/shard_map/ppermute | solution.py:334
  7.9 0.0 copy-done.2
  7.9 0.0 copy-done
  7.9 0.7 %shard_map.56 = (f32[8,8,128]{2,1,0:T(8,128)S(1)}, bf16[512,256]{1,0:T(8,128)(2,1)S(1)}) custom-call(f32[3,16]{1,0:T(4,128)S(1)} %bitcast.6, f32[16]{0:T(128)S(1)} %copy-done.2), custom_call_target="tpu_custom_call" | custom-call | tf_op jit(solution)/shard_map/pallas_call | solution.py:96
  8.5 0.0 collective-permute-done.high_ref
  8.6 0.3 collective-permute-done.1.low_ref
  8.9 0.0 copy-start.1
  8.9 13.0 %shard_map.57 = s32[3072,128]{1,0:T(8,128)S(1)} custom-call(bf16[10,96,2048]{2,1,0:T(8,128)(2,1)} %den_hbm.3, bf16[8,2048]{1,0:T(8,128)(2,1)S(1)} %collective-permute-done.high_ref, bf16[8,2048]{1,0:T(8,128)(2,1)S(1)} %collective-permute-done.1.low_ref, s32[8,96,2048]{2,1,0:T(8,128)} %mat_hbm.1, f32[8,8,128]{2,1,0:T(8,128)S(1)} %get-tuple-element.11.table, ...), custom_call_target="tpu_custom_call" | custom-call | tf_op jit(solution)/shard_map/pallas_call | solution.py:226
  21.9 31.2 %all_to_all.5 = s32[32,96,128]{2,1,0:T(8,128)S(1)} all-to-all(s32[32,96,128]{2,1,0:T(8,128)S(1)} %bitcast.5), channel_id=1, replica_groups=mesh['depth'=32,'screen'=8] {'depth'}, dimensions={0} | all-to-all | bytes 3145728 | tf_op jit(solution)/shard_map/all_to_all | solution.py:340
  53.1 0.0 copy-done.1
  53.1 1.9 %shard_map.58 = f32[3,4,2048]{2,1,0:T(4,128)} custom-call(s32[32]{0:T(128)S(1)} %copy-done.1, s32[32,3,2,16,128]{4,3,2,1,0:T(8,128)S(1)} %bitcast.4), custom_call_target="tpu_custom_call" | custom-call | tf_op jit(solution)/shard_map/pallas_call | solution.py:317
Async XLA Ops:
  0.0 7.9 %copy-start.2 = (f32[16]{0:T(128)S(1)}, f32[16]{0:T(128)}, u32[]{:S(2)}) copy-start(f32[16]{0:T(128)} %ext_ref.1) | copy-start | bytes 196
  0.0 7.9 %copy-start = (f32[16,3]{0,1:T(4,128)S(1)}, f32[16,3]{0,1:T(4,128)}, u32[]{:S(2)}) copy-start(f32[16,3]{0,1:T(4,128)} %param.8) | copy-start | bytes 580
  1.2 7.4 %collective-permute-start = (bf16[8,2048]{1,0:T(8,128)(2,1)S(1)}, bf16[8,2048]{1,0:T(8,128)(2,1)S(1)}, u32[]{:S(2)}, u32[]{:S(2)}) collective-permute-start(bf16[8,2048]{1,0:T(8,128)(2,1)S(1)} %get-tuple-element.9), channel_id=1, source_target_pairs={{1,0},{2,1},{3,2},{4,3},{5,4},{6,5},{7,6},{9,8},{10,9},{11,10},{12... | collective-permute-start | bytes 98312 | tf_op jit(solution)/shard_map/ppermute | solution.py:335
  3.1 5.8 %collective-permute-start.1 = (bf16[8,2048]{1,0:T(8,128)(2,1)S(1)}, bf16[8,2048]{1,0:T(8,128)(2,1)S(1)}, u32[]{:S(2)}, u32[]{:S(2)}) collective-permute-start(bf16[8,2048]{1,0:T(8,128)(2,1)S(1)} %get-tuple-element.10), channel_id=1, source_target_pairs={{0,1},{1,2},{2,3},{3,4},{4,5},{5,6},{6,7},{8,9},{9,10},{10,11},{11... | collective-permute-start | bytes 98312 | tf_op jit(solution)/shard_map/ppermute | solution.py:334
  8.9 44.2 %copy-start.1 = (s32[32]{0:T(128)S(1)}, s32[32]{0:T(128)}, u32[]{:S(2)}) copy-start(s32[32]{0:T(128)} %order_ref.1) | copy-start | bytes 388
